TPU v7x, 128 devices: a whole 4x4x4 slice. The times are simulated.
128 devices in a mesh: dp: 16 (over y, z), seq: 8 (over x, core).
Axes of the slice: x: 4, y: 4, z: 4, core: 2. Of those that a mesh axis runs over, the one named last changes fastest.
Arguments:
- tokens: bfloat16 [16384, 2880], P(('dp', 'seq')), may hold values from -6 to 6
- norm_gain: bfloat16 [2880], replicated, may hold values from 0.5 to 1.5
- router_weight: bfloat16 [2880, 64], replicated, may hold values from -0.109375 to 0.109375
- expert_ids: int32 [16384, 4], P(('dp', 'seq')), may hold values from 0 to 63, all different within a row; in each aligned block of 128 rows (0 to 127, 128 to 255, ...) at most 9 rows name the same one
- gate_up_words: int32 [128, 1440, 1440], P(('dp', 'seq')), may hold values from 0 to 255
- gate_up_scales: int32 [128, 90, 1440], P(('dp', 'seq')), may hold values from 119 to 121
- down_words: int32 [128, 720, 1440], P(('dp', 'seq')), may hold values from 0 to 255
- down_scales: int32 [128, 720, 90], P(('dp', 'seq')), may hold values from 119 to 121
- cotangent: bfloat16 [16384, 2880], P(('dp', 'seq')), may hold values from -6 to 6
Outputs:
- mixed: bfloat16 [16384, 2880], P(('dp', 'seq'))
- token_grad: bfloat16 [16384, 2880], P(('dp', 'seq'))
Inputs may be any that keep to these rules, and one draw needn't show every extreme that they name: `expert_ids`: in each device's aligned block of 128 tokens no expert is named more than 9 times, a bound that some block reaches.
All inputs are finite; a program needn't handle non-finite values.
Results may differ from a plain program's by a relative error of at most 0.0029.
Values may be sent and summed in bfloat16 or wider, within the bound.
No kernel may reach another device: no remote copies, remote signals or barrier semaphores. Data moves between devices by JAX's collectives and lax.ppermute only.
A program may use at most 192 MiB of HBM per device.

v0:
```python
import jax
import jax.numpy as jnp
from jax import lax
from jax.sharding import PartitionSpec as P

glu_slope = 1.702
norm_epsilon = 1e-05


def small_float(code_values):
    sign_part = code_values // 8
    level_code = code_values % 8
    exponent = level_code // 2
    mantissa = (level_code % 2).astype(jnp.float32)
    scaled = jnp.exp2((exponent - 1).astype(jnp.float32)) * (1.0 + 0.5 * mantissa)
    magnitude = jnp.where(exponent == 0, 0.5 * mantissa, scaled)
    return jnp.where(sign_part == 1, -magnitude, magnitude)


def unpack_rows(code_words, scale_codes):
    groups = scale_codes.shape[0]
    columns = code_words.shape[1]
    factor = jnp.exp2((scale_codes - 127).astype(jnp.float32))[:, None, :]
    shaped = code_words.reshape(groups, -1, columns)
    low_vals = (small_float(shaped % 16) * factor).astype(jnp.bfloat16)
    high_vals = (small_float(shaped // 16) * factor).astype(jnp.bfloat16)
    return jnp.stack([low_vals, high_vals], axis=2).reshape(-1, columns)


def unpack_cols(code_words, scale_codes):
    lines = code_words.shape[0]
    groups = scale_codes.shape[1]
    factor = jnp.exp2((scale_codes - 127).astype(jnp.float32))[:, :, None]
    shaped = code_words.reshape(lines, groups, -1)
    low_vals = (small_float(shaped % 16) * factor).astype(jnp.bfloat16)
    high_vals = (small_float(shaped // 16) * factor).astype(jnp.bfloat16)
    return jnp.stack([low_vals, high_vals], axis=3).reshape(lines, -1)


def expert_half(rows_in, grads_in, gate_up, down_proj):
    half_units = down_proj.shape[0]
    pre_act = jnp.dot(rows_in, gate_up, preferred_element_type=jnp.float32)
    gate_pre = pre_act[:, :half_units]
    up_pre = pre_act[:, half_units:]
    sig_gate = jax.nn.sigmoid(glu_slope * gate_pre)
    glu_gate = gate_pre * sig_gate
    active = (glu_gate * (up_pre + 1.0)).astype(jnp.bfloat16)
    part_out = jnp.dot(active, down_proj, preferred_element_type=jnp.float32).astype(jnp.bfloat16)
    back_act = lax.dot_general(
        grads_in, down_proj, (((1,), (1,)), ((), ())), preferred_element_type=jnp.float32
    )
    slope_term = sig_gate + glu_slope * glu_gate * (1.0 - sig_gate)
    grad_pre = jnp.concatenate(
        [back_act * (up_pre + 1.0) * slope_term, back_act * glu_gate], axis=1
    ).astype(jnp.bfloat16)
    part_back = lax.dot_general(
        grad_pre, gate_up, (((1,), (1,)), ((), ())), preferred_element_type=jnp.float32
    ).astype(jnp.bfloat16)
    return (part_out, part_back)


def shards(
    tokens,
    norm_gain,
    router_weight,
    expert_ids,
    gate_up_words,
    gate_up_scales,
    down_words,
    down_scales,
    cotangent,
):
    tok_count, width = tokens.shape
    top_count = expert_ids.shape[1]
    dp_count = lax.axis_size("dp")
    seq_count = lax.axis_size("seq")
    devices = dp_count * seq_count
    experts = devices // 2
    capacity = tok_count * top_count * 9 // (8 * experts)
    tok_f = tokens.astype(jnp.float32)
    cot_f = cotangent.astype(jnp.float32)
    gain_f = norm_gain.astype(jnp.float32)
    inv_rms = lax.rsqrt(jnp.mean(tok_f * tok_f, axis=1, keepdims=True) + norm_epsilon)
    normed = (tok_f * inv_rms * gain_f).astype(jnp.bfloat16)
    logits = jnp.dot(normed, router_weight, preferred_element_type=jnp.float32)
    expert_cols = lax.broadcasted_iota(jnp.int32, (tok_count, top_count, experts), 2)
    one_hot = expert_ids[:, :, None] == expert_cols
    picked = jnp.sum(jnp.where(one_hot, logits[:, None, :], 0.0), axis=2)
    raised = jnp.exp(picked)
    probs = raised / jnp.sum(raised, axis=1, keepdims=True)
    flat_probs = probs.reshape(-1)
    pair_count = tok_count * top_count
    flat_hot = one_hot.reshape(pair_count, experts).astype(jnp.int32)
    running = jnp.cumsum(flat_hot, axis=0)
    slot_of = jnp.sum(running * flat_hot, axis=1) - 1
    target = expert_ids.reshape(-1) * capacity + slot_of
    pair_index = jnp.arange(pair_count, dtype=jnp.int32)
    table = jnp.full((experts * capacity,), pair_count, jnp.int32).at[target].set(pair_index)
    filled = table < pair_count
    safe_pair = jnp.minimum(table, pair_count - 1)
    safe_token = safe_pair // top_count
    slot_rows = jnp.where(filled[:, None], normed[safe_token], 0)
    slot_grads = jnp.where(
        filled[:, None],
        (flat_probs[safe_pair][:, None] * cot_f[safe_token]).astype(jnp.bfloat16),
        0,
    )
    gate_up = unpack_rows(gate_up_words[0], gate_up_scales[0])
    down_proj = unpack_cols(down_words[0], down_scales[0])

    def spread(slot_values):
        return jnp.broadcast_to(
            slot_values.reshape(experts, 1, capacity, width), (experts, 2, capacity, width)
        ).reshape(devices, capacity, width)

    rows_in = lax.all_to_all(
        spread(slot_rows), ("dp", "seq"), split_axis=0, concat_axis=0, tiled=True
    )
    grads_in = lax.all_to_all(
        spread(slot_grads), ("dp", "seq"), split_axis=0, concat_axis=0, tiled=True
    )
    layout = rows_in.shape
    part_out, part_back = expert_half(
        rows_in.reshape(-1, width), grads_in.reshape(-1, width), gate_up, down_proj
    )
    part_out, part_back = (part_out.reshape(layout), part_back.reshape(layout))
    back_out, back_grad = (
        lax.all_to_all(part_out, ("dp", "seq"), split_axis=0, concat_axis=0, tiled=True),
        lax.all_to_all(part_back, ("dp", "seq"), split_axis=0, concat_axis=0, tiled=True),
    )
    out_slots = jnp.sum(
        back_out.reshape(experts, 2, capacity, width).astype(jnp.float32), axis=1
    ).reshape(experts * capacity, width)
    grad_slots = jnp.sum(
        back_grad.reshape(experts, 2, capacity, width).astype(jnp.float32), axis=1
    ).reshape(experts * capacity, width)
    pair_out = out_slots[target].reshape(tok_count, top_count, width)
    pair_back = grad_slots[target].reshape(tok_count, top_count, width)
    mixed = (tok_f + jnp.sum(probs[:, :, None] * pair_out, axis=1)).astype(jnp.bfloat16)
    dprob = jnp.sum(cot_f[:, None, :] * pair_out, axis=2)
    dpicked = probs * (dprob - jnp.sum(probs * dprob, axis=1, keepdims=True))
    dlogits = jnp.sum(jnp.where(one_hot, dpicked[:, :, None], 0.0), axis=1)
    dnormed = jnp.dot(
        dlogits, router_weight.astype(jnp.float32).T, precision=lax.Precision.HIGHEST
    ) + jnp.sum(pair_back, axis=1)
    gain_grad = gain_f * dnormed
    token_grad = (
        cot_f
        + inv_rms * gain_grad
        - tok_f * (inv_rms * inv_rms * inv_rms) * jnp.mean(gain_grad * tok_f, axis=1, keepdims=True)
    )
    return (mixed, token_grad.astype(jnp.bfloat16))


def solution(mesh):
    in_specs = (
        P(("dp", "seq"), None),
        P(),
        P(),
        P(("dp", "seq"), None),
        P(("dp", "seq"), None, None),
        P(("dp", "seq"), None, None),
        P(("dp", "seq"), None, None),
        P(("dp", "seq"), None, None),
        P(("dp", "seq"), None),
    )
    out_specs = (P(("dp", "seq"), None), P(("dp", "seq"), None))
    return jax.shard_map(shards, mesh=mesh, in_specs=in_specs, out_specs=out_specs, check_vma=False)
```

profile of v0, /device:TPU:74, one launch (start us, length us, event | category | flops | bytes accessed | tf_op | source)
XLA Modules:
  0.0 1136.7 jit_solution(363718618031563311)
XLA Ops:
  56.2 10.8 all-to-all-start
  67.9 182.3 %multiply_convert_fusion.2 = (bf16[90,16,1,1440]{3,2,1,0:T(2,128)(2,1)S(1)}, s32[90,16,1,1440]{3,2,1,0:T(1,128)S(1)}) fusion(f32[90,1440]{1,0:T(8,128)S(1)} %bitcast.52, s32[90,16,1,1440]{3,1,0,2:T(8,128)} %bitcast.47), kind=kLoop, calls=%fused_computation.46 | loop fusion | flops 130636800 | bytes 21254400 | tf_op jit(solution)/shard_map/convert_element_type | solution.py:25
  250.2 189.0 %multiply_convert_fusion.1 = bf16[90,16,1,1440]{3,2,1,0:T(2,128)(2,1)S(1)} fusion(s32[90,16,1,1440]{3,2,1,0:T(1,128)S(1)} %get-tuple-element.5, f32[90,1440]{1,0:T(8,128)S(1)} %bitcast.53, s32[90,16,1,1440]{3,1,0,2:T(8,128)} %bitcast.48), kind=kLoop, calls=%fused_computation.45 | loop fusion | flops 132710400 | bytes 21254400 | tf_op jit(solution)/shard_map/convert_element_type | solution.py:26
  439.3 21.7 %pad_maximum_fusion = bf16[90,16,2,1440]{3,2,1,0:T(2,128)(2,1)} fusion(bf16[90,16,1,1440]{3,2,1,0:T(2,128)(2,1)S(1)} %multiply_convert_fusion.1, bf16[90,16,1,1440]{3,2,1,0:T(2,128)(2,1)S(1)} %get-tuple-element.4), kind=kLoop, calls=%fused_computation.44 | loop fusion | flops 16588800 | bytes 16588800 | tf_op jit(solution)/shard_map/stack | solution.py:27
  461.0 18.6 %reshape.1154 = bf16[2880,1440]{1,0:T(8,128)(2,1)} reshape(bf16[90,16,2,1440]{3,2,1,0:T(2,128)(2,1)} %pad_maximum_fusion) | data formatting | bytes 16588800 | tf_op jit(solution)/shard_map/reshape | solution.py:27
  494.0 10.2 all-to-all-start.2
  504.1 24.1 %fusion.9 = (bf16[720,90,16,1]{0,2,1,3:T(8,128)(2,1)S(1)}, bf16[720,90,16,1]{0,2,1,3:T(8,128)(2,1)S(1)}) fusion(s32[720,90,16,1]{0,2,1,3:T(8,128)} %bitcast.49, f32[720,90]{0,1:T(8,128)S(1)} %bitcast.54), kind=kLoop, calls=%fused_computation.82 | loop fusion | flops 127526400 | bytes 8553600 | tf_op jit(solution)/shard_map/convert_element_type | solution.py:35
  540.4 10.1 reshape.1155
  550.5 13.9 %reshape.1153 = bf16[1152,2880]{1,0:T(8,128)(2,1)} reshape(bf16[128,9,2880]{2,1,0:T(8,128)(2,1)} %all-to-all-done) | data formatting | bytes 13271040 | tf_op jit(solution)/shard_map/reshape | solution.py:124
  564.4 18.1 %fusion.45 = f32[1152,1440]{0,1:T(8,128)} fusion(bf16[1152,2880]{1,0:T(8,128)(2,1)} %reshape.1153, bf16[2880,1440]{1,0:T(8,128)(2,1)} %reshape.1154), kind=kOutput, calls=%fused_computation.169 | convolution fusion | flops 9555148800 | bytes 21565440 | tf_op jit(solution)/shard_map/dot_general | solution.py:42
  582.5 81.3 %all-to-all-done.2 = bf16[128,9,2880]{2,1,0:T(8,128)(2,1)} async-done(((bf16[128,9,2880]{2,1,0:T(8,128)(2,1)}), bf16[128,9,2880]{2,1,0:T(8,128)(2,1)}, u32[]{:S(2)}, u32[]{:S(2)}) %all-to-all-start.2) | async-done | bytes 6635552 | tf_op jit(solution)/shard_map/all_to_all | solution.py:119
  663.7 13.9 %reshape.1160 = bf16[1152,2880]{1,0:T(8,128)(2,1)} reshape(bf16[128,9,2880]{2,1,0:T(8,128)(2,1)} %all-to-all-done.2) | data formatting | bytes 13271040 | tf_op jit(solution)/shard_map/reshape | solution.py:124
  677.7 12.5 %multiply_convert_fusion.4 = (bf16[1152,720]{0,1:T(8,128)(2,1)S(1)}, bf16[1152,720]{0,1:T(8,128)(2,1)S(1)}) fusion(f32[1152,1440]{0,1:T(8,128)} %fusion.45, bf16[1152,2880]{1,0:T(8,128)(2,1)} %reshape.1160, bf16[720,2880]{0,1:T(8,128)(2,1)} %reshape.1155), kind=kOutput, calls=%fused_computation.108 | convolution fusion | flops 4790016000 | bytes 20736000 | tf_op jit(solution)/shard_map/dot_general | solution.py:49
  690.3 13.3 %convolution_convert_fusion.1 = bf16[1152,2880]{0,1:T(8,128)(2,1)} fusion(bf16[2880,1440]{1,0:T(8,128)(2,1)S(1)} %bitcast.51, bf16[1152,720]{0,1:T(8,128)(2,1)S(1)} %get-tuple-element.7, bf16[1152,720]{0,1:T(8,128)(2,1)S(1)} %get-tuple-element.6), kind=kOutput, calls=%fused_computation.39 | convolution fusion | flops 9565102080 | bytes 18247680 | tf_op jit(solution)/shard_map/dot_general | solution.py:56
  703.6 10.1 copy.91
  713.7 13.1 %reshape.1161 = bf16[128,9,2880]{2,1,0:T(8,128)(2,1)} reshape(bf16[1152,2880]{1,0:T(8,128)(2,1)} %copy.91) | data formatting | bytes 13271040 | tf_op jit(solution)/shard_map/reshape | solution.py:126
  726.8 12.0 %all-to-all-start.3 = ((bf16[128,9,2880]{2,1,0:T(8,128)(2,1)}), bf16[128,9,2880]{2,1,0:T(8,128)(2,1)}, u32[]{:S(2)}, u32[]{:S(2)}) async-start(bf16[128,9,2880]{2,1,0:T(8,128)(2,1)} %reshape.1161), calls=%async_computation.3 | async-start | bytes 24117248 | tf_op jit(solution)/shard_map/all_to_all | solution.py:129
  738.8 11.6 %convolution_convert_fusion = bf16[1152,2880]{0,1:T(8,128)(2,1)} fusion(bf16[720,2880]{0,1:T(8,128)(2,1)} %reshape.1155, f32[1152,1440]{0,1:T(8,128)} %fusion.45), kind=kOutput, calls=%fused_computation.38 | convolution fusion | flops 4787527680 | bytes 17418240 | tf_op jit(solution)/shard_map/dot_general | solution.py:48
  760.5 13.2 %reshape.1156 = bf16[128,9,2880]{2,1,0:T(8,128)(2,1)} reshape(bf16[1152,2880]{1,0:T(8,128)(2,1)} %copy.84) | data formatting | bytes 13271040 | tf_op jit(solution)/shard_map/reshape | solution.py:126
  773.8 124.7 %all-to-all-done.3 = bf16[128,9,2880]{2,1,0:T(8,128)(2,1)} async-done(((bf16[128,9,2880]{2,1,0:T(8,128)(2,1)}), bf16[128,9,2880]{2,1,0:T(8,128)(2,1)}, u32[]{:S(2)}, u32[]{:S(2)}) %all-to-all-start.3) | async-done | bytes 6635552 | tf_op jit(solution)/shard_map/all_to_all | solution.py:129
  898.4 12.4 %all-to-all-start.1 = ((bf16[128,9,2880]{2,1,0:T(8,128)(2,1)}), bf16[128,9,2880]{2,1,0:T(8,128)(2,1)}, u32[]{:S(2)}, u32[]{:S(2)}) async-start(bf16[128,9,2880]{2,1,0:T(8,128)(2,1)} %reshape.1156), calls=%async_computation.1 | async-start | bytes 24117248 | tf_op jit(solution)/shard_map/all_to_all | solution.py:128
  910.8 16.0 %convert_reduce_fusion = f32[64,9,2880]{2,1,0:T(8,128)} fusion(bf16[128,9,2880]{2,1,0:T(8,128)(2,1)} %all-to-all-done.3), kind=kLoop, calls=%fused_computation.20 | loop fusion | flops 4976640 | bytes 13271040 | tf_op jit(solution)/shard_map/reduce_sum | solution.py:134
  961.6 113.9 %all-to-all-done.1 = bf16[128,9,2880]{2,1,0:T(8,128)(2,1)} async-done(((bf16[128,9,2880]{2,1,0:T(8,128)(2,1)}), bf16[128,9,2880]{2,1,0:T(8,128)(2,1)}, u32[]{:S(2)}, u32[]{:S(2)}) %all-to-all-start.1) | async-done | bytes 6635552 | tf_op jit(solution)/shard_map/all_to_all | solution.py:128
  1075.4 16.0 %convert_reduce_fusion.1 = f32[64,9,2880]{2,1,0:T(8,128)} fusion(bf16[128,9,2880]{2,1,0:T(8,128)(2,1)} %all-to-all-done.1), kind=kLoop, calls=%fused_computation.21 | loop fusion | flops 4976640 | bytes 13271040 | tf_op jit(solution)/shard_map/reduce_sum | solution.py:131
  (123 shorter events, 172.4 us)
Async XLA Ops:
  0.6 23.8 %copy-start = (bf16[2880,64]{0,1:T(8,128)(2,1)S(1)}, bf16[2880,64]{0,1:T(8,128)(2,1)}, u32[]{:S(2)}) copy-start(bf16[2880,64]{0,1:T(8,128)(2,1)} %param.11) | copy-start | bytes 1105924
  13.5 9.1 copy-start.20
  13.6 9.1 copy-start.3
  13.6 11.2 copy-start.14
  22.7 11.6 %copy-start.10 = (f32[2880]{0:T(1024)}, f32[2880]{0:T(1024)S(1)}, u32[]{:S(2)}) copy-start(f32[2880]{0:T(1024)S(1)} %convert_element_type.193) | copy-start | bytes 34564
  23.7 10.6 copy-start.21
  24.8 9.5 copy-start.16
  56.2 10.8 copy-start.8
  56.2 429.8 %all-to-all-start = ((bf16[128,9,2880]{2,1,0:T(8,128)(2,1)}), bf16[128,9,2880]{2,1,0:T(8,128)(2,1)}, u32[]{:S(2)}, u32[]{:S(2)}) async-start(bf16[128,9,2880]{2,1,0:T(8,128)(2,1)} %bitcast.45), calls=%async_computation | async-start | bytes 24117248 | tf_op jit(solution)/shard_map/all_to_all | solution.py:116
  494.0 169.8 %all-to-all-start.2 = ((bf16[128,9,2880]{2,1,0:T(8,128)(2,1)}), bf16[128,9,2880]{2,1,0:T(8,128)(2,1)}, u32[]{:S(2)}, u32[]{:S(2)}) async-start(bf16[128,9,2880]{2,1,0:T(8,128)(2,1)} %bitcast.46), calls=%async_computation.2 | async-start | bytes 24117248 | tf_op jit(solution)/shard_map/all_to_all | solution.py:119
  663.7 26.5 %slice-start = ((s8[8847360]{0:T(1024)(128)(4,1)}), s8[458752]{0:T(1024)(128)(4,1)S(1)}, s32[]{:S(2)}) async-start(s8[8847360]{0:T(1024)(128)(4,1)} %bitcast.50), calls=%async_computation.4 | async-start | bytes 917504
  677.7 12.6 %slice-start.1 = ((s8[8847360]{0:T(1024)(128)(4,1)}), s8[4194304]{0:T(1024)(128)(4,1)S(1)}, s32[]{:S(2)}) async-start(s8[8847360]{0:T(1024)(128)(4,1)} %bitcast.50), calls=%async_computation.5 | async-start | bytes 8388608
  677.7 12.6 %slice-start.2 = ((s8[8847360]{0:T(1024)(128)(4,1)}), s8[4194304]{0:T(1024)(128)(4,1)S(1)}, s32[]{:S(2)}) async-start(s8[8847360]{0:T(1024)(128)(4,1)} %bitcast.50), calls=%async_computation.6 | async-start | bytes 8388608
  726.8 171.6 %all-to-all-start.3 = ((bf16[128,9,2880]{2,1,0:T(8,128)(2,1)}), bf16[128,9,2880]{2,1,0:T(8,128)(2,1)}, u32[]{:S(2)}, u32[]{:S(2)}) async-start(bf16[128,9,2880]{2,1,0:T(8,128)(2,1)} %reshape.1161), calls=%async_computation.3 | async-start | bytes 24117248 | tf_op jit(solution)/shard_map/all_to_all | solution.py:129
  773.7 137.0 %copy-start.19 = (s32[512,1]{0,1:T(1,128)S(1)}, s32[512,1]{0,1:T(1,128)}, u32[]{:S(2)}) copy-start(s32[512,1]{0,1:T(1,128)} %copy-done.18) | copy-start | bytes 6148
  898.4 177.0 %all-to-all-start.1 = ((bf16[128,9,2880]{2,1,0:T(8,128)(2,1)}), bf16[128,9,2880]{2,1,0:T(8,128)(2,1)}, u32[]{:S(2)}, u32[]{:S(2)}) async-start(bf16[128,9,2880]{2,1,0:T(8,128)(2,1)} %reshape.1156), calls=%async_computation.1 | async-start | bytes 24117248 | tf_op jit(solution)/shard_map/all_to_all | solution.py:128
  1118.8 8.9 copy-start.13
  1118.8 8.9 copy-start.17
  1118.8 8.9 copy-start.15
  1118.8 9.0 copy-start.4
  1118.8 9.0 copy-start.11
  1118.9 14.4 %copy-start.5 = (bf16[128,2880]{0,1:T(8,128)(2,1)S(1)}, bf16[128,2880]{0,1:T(8,128)(2,1)}, u32[]{:S(2)}) copy-start(bf16[128,2880]{0,1:T(8,128)(2,1)} %param.17) | copy-start | bytes 2211844
  1118.9 14.4 %copy-start.22 = (f32[128]{0:T(128)S(1)}, f32[128]{0:T(128)}, u32[]{:S(2)}) copy-start(f32[128]{0:T(128)} %copy-done.21) | copy-start | bytes 1540
  1118.9 14.4 %copy-start.23 = (f32[128]{0:T(128)S(1)}, f32[128]{0:T(128)}, u32[]{:S(2)}) copy-start(f32[128]{0:T(128)} %get-tuple-element.16) | copy-start | bytes 1540
  (7 other events, 38.7 us)
where the time goes:
time: 1150 us; the launch traced here: 1140 us
  other arithmetic  484 us (42%)
  waiting for transfers between devices  320 us (28%)
  local copies, waits for them, and re-layouts  227 us (20%)
  matrix products  58.3 us (5%)
  starting transfers between devices  45.3 us (4%)
    convert_element_type x1, other arithmetic, unpack_rows(): high_vals = (small_float(shaped // 16) * factor).astype(jnp.bfloat16)  189 us
    convert_element_type x1, other arithmetic, unpack_rows(): low_vals = (small_float(shaped % 16) * factor).astype(jnp.bfloat16)  182 us
    all_to_all x1, waiting for transfers between devices, shards(): lax.all_to_all(part_back, ('dp', 'seq'), split_axis=0, concat_axis=0, til...  125 us
    all_to_all x1, waiting for transfers between devices, shards(): lax.all_to_all(part_out, ('dp', 'seq'), split_axis=0, concat_axis=0, tile...  114 us
    all_to_all x1, waiting for transfers between devices, shards(): lax.all_to_all(spread(slot_grads), ('dp', 'seq'), split_axis=0, concat_ax...  81.3 us
    reshape x2, local copies, waits for them, and re-layouts, shards(): part_out, part_back = (part_out.reshape(layout), part_back.reshape(layout))  26.4 us
    convert_element_type x1, other arithmetic, unpack_cols(): low_vals = (small_float(shaped % 16) * factor).astype(jnp.bfloat16)  24.1 us
  transfers between devices with their start and end apart: 4, of which 3 were waited for; matrix products, arithmetic and copies ran while one was open for 51% of the time, Pallas kernels for 0%

commit v1 on v0

v1 whole, which is shorter than its diff:
```python
import functools

import jax
import jax.numpy as jnp
from jax import lax
from jax.experimental import pallas as pl
from jax.experimental.pallas import tpu as pltpu
from jax.sharding import Mesh, PartitionSpec as P

glu_slope = 1.702
norm_epsilon = 1e-05

LANE = 128
PAIR = 2 * LANE
SLOTS = 8
F32 = jnp.float32
BF16 = jnp.bfloat16


def up_to(n, m):
    return -(-n // m) * m


def mm(a, b):
    return jnp.dot(a, b, preferred_element_type=F32)


def mm_nt(a, b):
    return lax.dot_general(a, b, (((1,), (1,)), ((), ())), preferred_element_type=F32)


def iota(shape, dim):
    return lax.broadcasted_iota(jnp.int32, shape, dim)


def mm_tn(a, b):
    return lax.dot_general(a, b, (((0,), (0,)), ((), ())), preferred_element_type=F32)


def split_matrix(n):
    nat, col = iota((n, n), 0), iota((n, n), 1)
    half = n // 2
    src = jnp.where(col < half, 2 * col, 2 * (col - half) + 1)
    return (nat == src).astype(F32).astype(BF16)


def feature_blocks(width):
    full = width // PAIR * PAIR
    blocks = [(start, PAIR, split_matrix(PAIR)) for start in range(0, full, PAIR)]
    return blocks + ([(full, width - full, split_matrix(width - full))] if width > full else [])


def order_columns(src_ref, dst_ref):
    for start, size, hot in feature_blocks(src_ref.shape[1]):
        dst_ref[:, start : start + size] = mm(src_ref[:, start : start + size], hot).astype(BF16)


def order_rows(src_ref, dst_ref):
    for start, size, hot in feature_blocks(src_ref.shape[0]):
        dst_ref[:, start : start + size] = mm_tn(src_ref[start : start + size, :], hot).astype(BF16)


def restore_rows(load, dst_ref):
    for start, size, hot in feature_blocks(dst_ref.shape[0]):
        dst_ref[start : start + size, :] = mm_nt(hot, load(start, size)).astype(BF16)


def tail_geometry(width):
    tail_at = up_to(width, LANE)
    tail = up_to(-(-tail_at // SLOTS), LANE)
    return tail_at, tail


def slot_hot(slot_t):
    experts, toks = slot_t.shape
    s_idx = iota((experts, SLOTS, toks), 1).astype(F32)
    hot = (slot_t[:, None, :] == s_idx).astype(F32)
    return hot.reshape(experts * SLOTS, toks), (slot_t == float(SLOTS)).astype(F32)


def put_tail(msg_ref, nine, nine_sc, fold_sc, tail_at, tail, width):
    experts = nine.shape[0]
    nine_sc[:, width:] = jnp.zeros((experts, nine_sc.shape[1] - width), F32)
    nine_sc[:, :width] = nine
    fold_lanes(msg_ref, nine_sc, fold_sc, experts, tail_at, tail)


def fold_lanes(msg_ref, nine, fold_sc, experts, tail_at, tail):
    for j in range(tail // LANE):
        for r in range(SLOTS):
            at = r * tail + j * LANE
            fold_sc[j, pl.ds(r, experts, stride=SLOTS), :] = nine[:, at : at + LANE]
        at = tail_at + j * LANE
        msg_ref[:, at : at + LANE] = fold_sc[j].astype(BF16)


def get_tail(msg_ref, fold_sc, put, tail_at, tail, experts):
    for j in range(tail // LANE):
        at = tail_at + j * LANE
        fold_sc[j] = msg_ref[:, at : at + LANE].astype(F32)
        for r in range(SLOTS):
            put(r * tail + j * LANE, fold_sc[j, pl.ds(r, experts, stride=SLOTS), :].astype(BF16))


def dispatch_rows_kernel(
    tok_ref, gain_ref, router_ref, ids_ref,
    msg_ref, prob_ref, slot_ref, tokp_ref, gainp_ref, routerp_ref,
    normp_sc, gain_sc, nine_sc, fold_sc,
):
    width, toks = tok_ref.shape
    top = ids_ref.shape[0]
    experts = router_ref.shape[0]
    tail_at, tail = tail_geometry(width)
    order_rows(tok_ref, tokp_ref)
    gain_sc[...] = jnp.broadcast_to(gain_ref[...], gain_sc.shape)
    order_columns(gain_sc, gainp_ref)
    order_columns(router_ref, routerp_ref)
    tok = tokp_ref[...].astype(F32)
    inv = lax.rsqrt(jnp.sum(tok * tok, axis=1, keepdims=True) / width + norm_epsilon)
    normp_sc[...] = (tok * inv * gainp_ref[0:1, :].astype(F32)).astype(BF16)
    logits = mm_nt(routerp_ref[...], normp_sc[...])
    e_idx = iota((experts, toks), 0)
    chosen = e_idx == ids_ref[0:1, :]
    for k in range(1, top):
        chosen = chosen | (e_idx == ids_ref[k : k + 1, :])
    raised = jnp.where(chosen, jnp.exp(logits), 0.0)
    prob_ref[...] = raised / jnp.sum(raised, axis=0, keepdims=True)
    earlier = (iota((toks, toks), 0) < iota((toks, toks), 1)).astype(F32).astype(BF16)
    rank = mm(chosen.astype(F32).astype(BF16), earlier)
    slot = jnp.where(chosen, rank, -1.0)
    slot_ref[...] = slot
    hot, hot_nine = slot_hot(slot)
    hot = hot.astype(BF16)
    for start in range(0, width, 2 * PAIR):
        stop = min(start + 2 * PAIR, width)
        msg_ref[:, start:stop] = mm(hot, normp_sc[:, start:stop]).astype(BF16)
    msg_ref[:, width:tail_at] = jnp.zeros((msg_ref.shape[0], tail_at - width), BF16)
    nine = mm(hot_nine.astype(BF16), normp_sc[...])
    put_tail(msg_ref, nine, nine_sc, fold_sc, tail_at, tail, width)


def dispatch_grads_kernel(
    cot_ref, prob_ref, slot_ref,
    msg_ref, cotp_ref,
    nine_sc, fold_sc,
):
    width, toks = cot_ref.shape
    experts = prob_ref.shape[0]
    tail_at, tail = tail_geometry(width)
    order_rows(cot_ref, cotp_ref)
    prob = prob_ref[...]
    hot, hot_nine = slot_hot(slot_ref[...])
    spread = jnp.broadcast_to(prob[:, None, :], (experts, SLOTS, toks)).reshape(experts * SLOTS, toks)
    row_prob = jnp.sum(hot * spread, axis=1, keepdims=True)
    nine_prob = jnp.sum(hot_nine * prob, axis=1, keepdims=True)
    hot = hot.astype(BF16)
    for start in range(0, width, 2 * PAIR):
        stop = min(start + 2 * PAIR, width)
        msg_ref[:, start:stop] = (mm(hot, cotp_ref[:, start:stop]) * row_prob).astype(BF16)
    msg_ref[:, width:tail_at] = jnp.zeros((msg_ref.shape[0], tail_at - width), BF16)
    nine = mm(hot_nine.astype(BF16), cotp_ref[...]) * nine_prob
    put_tail(msg_ref, nine, nine_sc, fold_sc, tail_at, tail, width)


def code_value(code):
    m = code & 7
    mag = jnp.maximum(jnp.maximum(m, 2 * m - 4), 4 * m - 16)
    return jnp.where((code & 8) != 0, -mag, mag).astype(F32)


def decode_rows_kernel(rest, words_ref, scales_ref, out_ref, factor_sc):
    groups = scales_ref.shape[0]
    columns = words_ref.shape[1]
    out_ref[:, columns:] = jnp.zeros((out_ref.shape[0], out_ref.shape[1] - columns), BF16)
    per = words_ref.shape[0] // groups
    step = pl.program_id(0)
    last = pl.num_programs(0) - 1
    factor_sc[...] = jnp.exp2((scales_ref[...] - 128).astype(F32))

    def group(g, low_at, high_at):
        for start in range(0, columns, 4 * LANE):
            stop = min(start + 4 * LANE, columns)
            w = words_ref[g * per : (g + 1) * per, start:stop]
            f = factor_sc[g : g + 1, start:stop]
            out_ref[low_at : low_at + per, start:stop] = (code_value(w) * f).astype(BF16)
            out_ref[high_at : high_at + per, start:stop] = (code_value(w >> 4) * f).astype(BF16)

    @pl.when(step < last)
    def _():
        for g in range(groups):
            group(g, g * per, LANE + g * per)

    @pl.when(step == last)
    def _():
        for g in range(rest // per):
            group(g, g * per, rest + g * per)


def decode_cols_kernel(words_ref, scales_ref, out_ref, factor_sc):
    rows, columns = words_ref.shape
    groups = scales_ref.shape[1]
    per = columns // groups
    step_rows = 16
    expand = (iota((groups, columns), 0) == iota((groups, columns), 1) // per).astype(F32).astype(BF16)
    factor_sc[...] = mm(jnp.exp2((scales_ref[...] - 128).astype(F32)).astype(BF16), expand)
    full = columns // LANE * LANE
    rest = columns - full

    def body(i, carry):
        r = pl.ds(pl.multiple_of(i * step_rows, step_rows), step_rows)
        for start in range(0, full, LANE):
            w = words_ref[r, start : start + LANE]
            f = factor_sc[r, start : start + LANE]
            out_ref[r, 2 * start : 2 * start + LANE] = (code_value(w) * f).astype(BF16)
            out_ref[r, 2 * start + LANE : 2 * start + PAIR] = (code_value(w >> 4) * f).astype(BF16)
        if rest:
            w = words_ref[r, full:columns]
            f = factor_sc[r, full:columns]
            both = jnp.concatenate([code_value(w) * f, code_value(w >> 4) * f], axis=1)
            out_ref[r, 2 * full :] = both.astype(BF16)
        return carry

    lax.fori_loop(0, rows // step_rows, body, 0)


def rounded(half_sum):
    return half_sum.astype(BF16).astype(F32)


def ffn_forward_kernel(
    x_ref, gu_own_ref, gu_oth_ref, down_own_ref, down_oth_ref,
    out_ref, coef_own_ref, coef_oth_ref,
    x_sc, pre_sc, act_own_sc, act_oth_sc, res_sc, fold_sc,
    *, width, half, n_up, n_down,
):
    step = pl.program_id(0)
    rows = x_ref.shape[0]
    experts = rows // SLOTS
    all_rows = rows + experts
    tail_at, tail = tail_geometry(width)
    tile_up = gu_own_ref.shape[1]
    tile_down = down_own_ref.shape[1]
    padded = pre_sc.shape[1]

    @pl.when(step == 0)
    def _():
        x_sc[:rows, :width] = x_ref[:, :width]

        def put(at, value):
            x_sc[rows:, at : at + LANE] = value

        get_tail(x_ref, fold_sc, put, tail_at, tail, experts)

    def up(gu_ref, index):
        at = pl.multiple_of(index * tile_up, tile_up)
        pre_sc[:, pl.ds(at, tile_up)] = mm(x_sc[:, :width], gu_ref[...])

    def finish(act_sc, coef_ref):
        chunk = 16

        def body(i, carry):
            r = pl.ds(pl.multiple_of(i * chunk, chunk), chunk)
            pre = pre_sc[r, :]
            wide = act_sc.shape[1]
            gate = pre[:, :wide]
            lift = pltpu.roll(pre, padded - half, 1)[:, :wide] + 1.0
            sig = jax.nn.sigmoid(glu_slope * gate)
            glu = gate * sig
            act_sc[r, :] = (glu * lift).astype(BF16)
            slope = sig + glu_slope * glu * (1.0 - sig)
            grad_gate = lift * slope
            zero = jnp.zeros((chunk, padded - wide), F32)
            grad_up = pltpu.roll(jnp.concatenate([glu, zero], axis=1), half, 1)
            lanes = iota((chunk, padded), 1)
            coef_ref[r, :] = jnp.where(
                lanes < half, jnp.concatenate([grad_gate, zero], axis=1), grad_up
            )
            return carry

        lax.fori_loop(0, all_rows // chunk, body, 0)

    @pl.when(step < n_up)
    def _():
        up(gu_own_ref, step)

    @pl.when(step == n_up - 1)
    def _():
        finish(act_own_sc, coef_own_ref)

    @pl.when((step >= n_up) & (step < 2 * n_up))
    def _():
        up(gu_oth_ref, step - n_up)

    @pl.when(step == 2 * n_up - 1)
    def _():
        finish(act_oth_sc, coef_oth_ref)

    @pl.when(step >= 2 * n_up)
    def _():
        at = pl.multiple_of((step - 2 * n_up) * tile_down, tile_down)
        res_sc[:, pl.ds(at, tile_down)] = rounded(
            mm(act_own_sc[:, :half], down_own_ref[...])
        ) + rounded(mm(act_oth_sc[:, :half], down_oth_ref[...]))

    @pl.when(step == 2 * n_up + n_down - 1)
    def _():
        emit(out_ref, res_sc, fold_sc, rows, experts, tail_at, tail)


def emit(out_ref, res_sc, fold_sc, rows, experts, tail_at, tail):
    chunk = 32

    def body(i, carry):
        r = pl.ds(pl.multiple_of(i * chunk, chunk), chunk)
        out_ref[r, :tail_at] = res_sc[r, :tail_at].astype(BF16)
        return carry

    lax.fori_loop(0, rows // chunk, body, 0)
    fold_lanes(out_ref, res_sc.at[rows:, :], fold_sc, experts, tail_at, tail)


def ffn_backward_kernel(
    g_ref, coef_own_ref, coef_oth_ref, down_own_ref, down_oth_ref, gu_own_ref, gu_oth_ref,
    out_ref,
    g_sc, back_sc, pre_own_sc, pre_oth_sc, res_sc, fold_sc,
    *, width, half, inner, n_back,
):
    step = pl.program_id(0)
    rows = g_ref.shape[0]
    experts = rows // SLOTS
    all_rows = rows + experts
    tail_at, tail = tail_geometry(width)
    tile = gu_own_ref.shape[0]
    padded = coef_own_ref.shape[1]

    @pl.when(step == 0)
    def _():
        g_sc[:rows, :width] = g_ref[:, :width]

        def put(at, value):
            g_sc[rows:, at : at + LANE] = value

        get_tail(g_ref, fold_sc, put, tail_at, tail, experts)

    def finish(coef_ref, pre_sc):
        chunk = 16

        def body(i, carry):
            r = pl.ds(pl.multiple_of(i * chunk, chunk), chunk)
            back = back_sc[r, :]
            lanes = iota((chunk, padded), 1)
            twice = jnp.where(lanes < half, back, pltpu.roll(back, half, 1))
            pre_sc[r, :] = (twice * coef_ref[r, :]).astype(BF16)
            return carry

        lax.fori_loop(0, all_rows // chunk, body, 0)

    @pl.when(step == 0)
    def _():
        back_sc[:, :half] = mm_nt(g_sc[:, :width], down_own_ref[...])
        finish(coef_own_ref, pre_own_sc)

    @pl.when(step == 1)
    def _():
        back_sc[:, :half] = mm_nt(g_sc[:, :width], down_oth_ref[...])
        finish(coef_oth_ref, pre_oth_sc)

    @pl.when(step >= 2)
    def _():
        at = pl.multiple_of((step - 2) * tile, tile)
        res_sc[:, pl.ds(at, tile)] = rounded(
            mm_nt(pre_own_sc[:, :inner], gu_own_ref[:, :inner])
        ) + rounded(mm_nt(pre_oth_sc[:, :inner], gu_oth_ref[:, :inner]))

    @pl.when(step == 2 + n_back - 1)
    def _():
        emit(out_ref, res_sc, fold_sc, rows, experts, tail_at, tail)


def combine_out_kernel(
    msg_ref, tokp_ref, cotp_ref, prob_ref, slot_ref, router_ref,
    mixed_ref, dnormed_ref,
    nine_sc, fold_sc, mix_sc,
):
    toks, width = tokp_ref.shape
    experts = prob_ref.shape[0]
    tail_at, tail = tail_geometry(width)

    def put(at, value):
        nine_sc[:, at : at + LANE] = value

    get_tail(msg_ref, fold_sc, put, tail_at, tail, experts)
    prob = prob_ref[...]
    hot, hot_nine = slot_hot(slot_ref[...])
    spread = jnp.broadcast_to(prob[:, None, :], (experts, SLOTS, toks)).reshape(experts * SLOTS, toks)
    weight = jnp.concatenate([hot * spread, hot_nine * prob], axis=0).T
    high = weight.astype(BF16)
    low = (weight - high.astype(F32)).astype(BF16)
    main = experts * SLOTS
    for start in range(0, width, 2 * PAIR):
        stop = min(start + 2 * PAIR, width)
        rows = msg_ref[:, start:stop]
        nine = nine_sc[:, start:stop]
        total = tokp_ref[:, start:stop].astype(F32)
        total = total + mm(high[:, :main], rows) + mm(low[:, :main], rows)
        total = total + mm(high[:, main:], nine) + mm(low[:, main:], nine)
        mix_sc[:, start:stop] = total.astype(BF16)

    restore_rows(lambda start, size: mix_sc[:, start : start + size], mixed_ref)
    cot = cotp_ref[...]
    along = (mm_nt(msg_ref[:, :width], cot) * hot).reshape(experts, SLOTS, toks)
    dprob = jnp.sum(along, axis=1) + mm_nt(nine_sc[:, :width], cot) * hot_nine
    dlogits_t = prob * (dprob - jnp.sum(prob * dprob, axis=0, keepdims=True))
    dlogits = dlogits_t.T
    first = dlogits.astype(BF16)
    left = dlogits - first.astype(F32)
    second = left.astype(BF16)
    third = (left - second.astype(F32)).astype(BF16)
    router = router_ref[...]
    dnormed_ref[...] = mm(first, router) + mm(second, router) + mm(third, router)


def combine_back_kernel(
    msg_ref, tokp_ref, cotp_ref, slot_ref, gain_ref, dnormed_ref,
    grad_ref,
    nine_sc, fold_sc, sum_sc,
):
    toks, width = tokp_ref.shape
    experts = slot_ref.shape[0]
    tail_at, tail = tail_geometry(width)

    def put(at, value):
        nine_sc[:, at : at + LANE] = value

    get_tail(msg_ref, fold_sc, put, tail_at, tail, experts)
    hot, hot_nine = slot_hot(slot_ref[...])
    pick = jnp.concatenate([hot, hot_nine], axis=0).T.astype(BF16)
    main = experts * SLOTS
    tok = tokp_ref[...].astype(F32)
    inv = lax.rsqrt(jnp.sum(tok * tok, axis=1, keepdims=True) / width + norm_epsilon)
    along = jnp.zeros((toks, 1), F32)
    for start in range(0, width, 2 * PAIR):
        stop = min(start + 2 * PAIR, width)
        total = mm(pick[:, :main], msg_ref[:, start:stop]) + mm(pick[:, main:], nine_sc[:, start:stop])
        total = (total + dnormed_ref[:, start:stop]) * gain_ref[0:1, start:stop].astype(F32)
        sum_sc[:, start:stop] = total
        along = along + jnp.sum(total * tokp_ref[:, start:stop].astype(F32), axis=1, keepdims=True)
    cube = inv * inv * inv * (along / width)

    def load(start, size):
        value = (
            cotp_ref[:, start : start + size].astype(F32)
            + inv * sum_sc[:, start : start + size]
            - tokp_ref[:, start : start + size].astype(F32) * cube
        )
        return value.astype(BF16)

    restore_rows(load, grad_ref)


def params(mib):
    return pltpu.CompilerParams(vmem_limit_bytes=mib * 1024 * 1024)


def once(shape):
    return pl.BlockSpec(shape, lambda *_: (0,) * len(shape), pipeline_mode=pl.Buffered(1))


def simple_call(kernel, outs, scratch):
    return pl.pallas_call(
        kernel, out_shape=outs, scratch_shapes=scratch, compiler_params=params(24)
    )


def struct(shape, dtype):
    return jax.ShapeDtypeStruct(shape, dtype)


def shards(
    tokens, norm_gain, router_weight, expert_ids,
    gate_up_words, gate_up_scales, down_words, down_scales, cotangent,
):
    toks, width = tokens.shape
    experts = router_weight.shape[1]
    word_rows, inner = gate_up_words.shape[1:]
    half, word_cols = down_words.shape[1:]
    tail_at, tail = tail_geometry(width)
    msg_width = tail_at + tail
    rows = experts * SLOTS
    all_rows = rows + experts
    wide = SLOTS * tail
    padded = up_to(inner, PAIR)
    gain = norm_gain.reshape(1, width)

    nine_f = pltpu.VMEM((experts, wide), F32)
    nine_b = pltpu.VMEM((experts, wide), BF16)
    fold = pltpu.VMEM((tail // LANE, rows, LANE), F32)
    msg = struct((rows, msg_width), BF16)

    table = struct((experts, toks), F32)
    block = struct((toks, width), BF16)
    row_msg, prob, slot, tokp, gainp, routerp = simple_call(
        dispatch_rows_kernel,
        (msg, table, table, block, struct((16, width), BF16), struct((experts, width), BF16)),
        [pltpu.VMEM((toks, width), BF16), pltpu.VMEM((16, width), BF16), nine_f, fold],
    )(tokens.T, gain, router_weight.T, expert_ids.T)
    row_msg, gate_up_words, down_words = lax.optimization_barrier(
        (row_msg, gate_up_words, down_words)
    )

    def exchange(message):
        shaped = message.reshape(experts, SLOTS, msg_width)
        swapped = lax.all_to_all(shaped, ("dp", "x"), 0, 0, tiled=True)
        return swapped.reshape(rows, msg_width)

    rows_in = exchange(row_msg)
    grad_msg, cotp = simple_call(
        dispatch_grads_kernel, (msg, block), [nine_f, fold]
    )(cotangent.T, prob, slot)
    grads_in = exchange(grad_msg)

    group_rows = word_rows // gate_up_scales.shape[1]
    steps = -(-word_rows // LANE)
    gate_up = pl.pallas_call(
        functools.partial(decode_rows_kernel, word_rows - (steps - 1) * LANE),
        out_shape=struct((2 * word_rows, padded), BF16),
        grid=(steps,),
        in_specs=[
            pl.BlockSpec((LANE, inner), lambda i: (i, 0)),
            pl.BlockSpec((LANE // group_rows, inner), lambda i: (i, 0)),
        ],
        out_specs=pl.BlockSpec((PAIR, padded), lambda i: (i, 0)),
        scratch_shapes=[pltpu.VMEM((LANE // group_rows, inner), F32)],
        compiler_params=params(24),
        name="decode_gate_up",
    )(gate_up_words[0], gate_up_scales[0])
    down_rows = 144
    down = pl.pallas_call(
        decode_cols_kernel,
        out_shape=struct((half, 2 * word_cols), BF16),
        grid=(half // down_rows,),
        in_specs=[
            pl.BlockSpec((down_rows, word_cols), lambda i: (i, 0)),
            pl.BlockSpec((down_rows, down_scales.shape[2]), lambda i: (i, 0)),
        ],
        out_specs=pl.BlockSpec((down_rows, 2 * word_cols), lambda i: (i, 0)),
        scratch_shapes=[pltpu.VMEM((down_rows, word_cols), F32)],
        compiler_params=params(24),
        name="decode_down",
    )(down_words[0], down_scales[0])
    swap = [(0, 1), (1, 0)]
    gate_up_other = lax.ppermute(gate_up, "core", swap)
    down_other = lax.ppermute(down, "core", swap)

    tile = 512
    n_up = -(-inner // tile)
    n_down = -(-width // tile)
    half_wide = up_to(half, LANE)
    coef = struct((all_rows, padded), F32)

    def clip(i, low, count):
        return jnp.clip(i - low, 0, count - 1)

    out_msg, coef_own, coef_oth = pl.pallas_call(
        functools.partial(ffn_forward_kernel, width=width, half=half, n_up=n_up, n_down=n_down),
        out_shape=(msg, coef, coef),
        grid=(2 * n_up + n_down,),
        in_specs=[
            once((rows, msg_width)),
            pl.BlockSpec((width, tile), lambda i: (0, clip(i, 0, n_up))),
            pl.BlockSpec((width, tile), lambda i: (0, clip(i, n_up, n_up))),
            pl.BlockSpec((half, tile), lambda i: (0, clip(i, 2 * n_up, n_down))),
            pl.BlockSpec((half, tile), lambda i: (0, clip(i, 2 * n_up, n_down))),
        ],
        out_specs=(once((rows, msg_width)), once((all_rows, padded)), once((all_rows, padded))),
        scratch_shapes=[
            pltpu.VMEM((all_rows, wide), BF16),
            pltpu.VMEM((all_rows, padded), F32),
            pltpu.VMEM((all_rows, half_wide), BF16),
            pltpu.VMEM((all_rows, half_wide), BF16),
            pltpu.VMEM((all_rows, n_down * tile), F32),
            fold,
        ],
        compiler_params=params(52),
        name="ffn_forward",
    )(rows_in, gate_up, gate_up_other, down, down_other)
    outs_in = exchange(out_msg)

    back_msg = pl.pallas_call(
        functools.partial(
            ffn_backward_kernel, width=width, half=half, inner=inner, n_back=n_down
        ),
        out_shape=msg,
        grid=(2 + n_down,),
        in_specs=[
            once((rows, msg_width)),
            once((all_rows, padded)),
            once((all_rows, padded)),
            once((half, width)),
            once((half, width)),
            pl.BlockSpec((tile, padded), lambda i: (clip(i, 2, n_down), 0)),
            pl.BlockSpec((tile, padded), lambda i: (clip(i, 2, n_down), 0)),
        ],
        out_specs=once((rows, msg_width)),
        scratch_shapes=[
            pltpu.VMEM((all_rows, wide), BF16),
            pltpu.VMEM((all_rows, padded), F32),
            pltpu.VMEM((all_rows, padded), BF16),
            pltpu.VMEM((all_rows, padded), BF16),
            pltpu.VMEM((all_rows, n_down * tile), F32),
            fold,
        ],
        compiler_params=params(52),
        name="ffn_backward",
    )(grads_in, coef_own, coef_oth, down, down_other, gate_up, gate_up_other)
    backs_in = exchange(back_msg)

    turned = struct((width, toks), BF16)
    mixed, dnormed = simple_call(
        combine_out_kernel,
        (turned, struct((toks, width), F32)),
        [nine_b, fold, pltpu.VMEM((toks, width), BF16)],
    )(outs_in, tokp, cotp, prob, slot, routerp)
    token_grad = simple_call(
        combine_back_kernel, turned, [nine_b, fold, pltpu.VMEM((toks, width), F32)]
    )(backs_in, tokp, cotp, slot, gainp, dnormed)
    return mixed.T, token_grad.T


def solution(mesh):
    dp, seq = mesh.devices.shape
    split = Mesh(mesh.devices.reshape(dp, seq // 2, 2), ("dp", "x", "core"))
    every = ("dp", "x", "core")
    flat, deep = P(every, None), P(every, None, None)
    return jax.shard_map(
        shards,
        mesh=split,
        in_specs=(flat, P(), P(), flat, deep, deep, deep, deep, flat),
        out_specs=(flat, flat),
        check_vma=False,
    )
```

time: 1150 us -> 244 us (0.21)
  the two profiles are of different devices: /device:TPU:74 before, /device:TPU:0 now
where the time goes in v1:
time: 244 us; the launch traced here: 243 us
  Pallas kernels  105 us (43%)
  waiting for transfers between devices  86.1 us (35%)
  starting transfers between devices  28.1 us (12%)
  local copies, waits for them, and re-layouts  23 us (9%)
    all_to_all x4, waiting for transfers between devices, exchange(): swapped = lax.all_to_all(shaped, ('dp', 'x'), 0, 0, tiled=True)  86 us
    pallas_call x1, Pallas kernels, shards(): pl.pallas_call(functools.partial(ffn_forward_kernel, width=width, half=ha...  36 us
    pallas_call x1, Pallas kernels, shards(): pl.pallas_call(functools.partial(ffn_backward_kernel, width=width, half=h...  34.6 us
    all_to_all x4, starting transfers between devices, exchange(): swapped = lax.all_to_all(shaped, ('dp', 'x'), 0, 0, tiled=True)  27.9 us
    unnamed x42, local copies, waits for them, and re-layouts  22.3 us
    pallas_call x1, Pallas kernels, shards(): pl.pallas_call(functools.partial(decode_rows_kernel, word_rows - (steps -...  10.5 us
    pallas_call x1, Pallas kernels, shards(): pl.pallas_call(decode_cols_kernel, out_shape=struct((half, 2 * word_cols)...  7.39 us
  transfers between devices with their start and end apart: 6, of which 4 were waited for; matrix products, arithmetic and copies ran while one was open for 0% of the time, Pallas kernels for 35%

profile of v1, /device:TPU:0, one launch (start us, length us, event | category | flops | bytes accessed | tf_op | source)
XLA Modules:
  0.0 243.1 jit_solution(15335177029260751779)
XLA Ops:
  4.1 4.1 %shard_map.104 = (bf16[512,3328]{1,0:T(8,128)(2,1)}, f32[64,128]{1,0:T(8,128)S(1)}, f32[64,128]{1,0:T(8,128)S(1)}, bf16[128,2880]{1,0:T(8,128)(2,1)S(1)}, bf16[1...) custom-call(bf16[2880,128]{1,0:T(8,128)(2,1)S(1)} %bitcast.25, bf16[1,2880]{1,0:T(2,128)(2,1)S(1)} %reshape.31.gain_ref, ...), custom_call_target="tpu_custom_call" | custom-call | tf_op jit(solution)/shard_map/pallas_call | solution.py:502
  8.8 1.5 copy.14
  10.4 3.5 %copy-done = s32[1,1440,1440]{2,1,0:T(8,128)S(1)} copy-done((s32[1,1440,1440]{2,1,0:T(8,128)S(1)}, s32[1,1440,1440]{2,1,0:T(8,128)}, u32[]{:S(2)}) %copy-start) | copy-done | bytes 8294424
  13.9 10.5 %decode_gate_up.1.gu_own_ref = bf16[2880,1536]{1,0:T(8,128)(2,1)} custom-call(s32[1440,1440]{1,0:T(8,128)S(1)} %bitcast.21, s32[90,1440]{1,0:T(8,128)S(1)} %bitcast.23), custom_call_target="tpu_custom_call" | custom-call | tf_op jit(solution)/shard_map/decode_gate_up/pallas_call | solution.py:524
  24.4 11.9 %all-to-all-start = ((bf16[64,8,3328]{2,1,0:T(8,128)(2,1)}), bf16[64,8,3328]{2,1,0:T(8,128)(2,1)}, u32[]{:S(2)}, u32[]{:S(2)}) async-start(bf16[64,8,3328]{2,1,0:T(8,128)(2,1)} %bitcast.3), calls=%async_computation | async-start | bytes 6815744 | tf_op jit(solution)/shard_map/all_to_all | solution.py:513
  36.5 2.2 copy-done.1
  38.8 7.4 %decode_down.1.down_own_ref = bf16[720,2880]{1,0:T(8,128)(2,1)} custom-call(s32[720,1440]{1,0:T(8,128)S(1)} %bitcast.22, s32[720,90]{1,0:T(8,128)S(1)} %bitcast.24), custom_call_target="tpu_custom_call" | custom-call | tf_op jit(solution)/shard_map/decode_down/pallas_call | solution.py:538
  46.4 3.2 %shard_map.105 = (bf16[512,3328]{1,0:T(8,128)(2,1)}, bf16[128,2880]{1,0:T(8,128)(2,1)S(1)}) custom-call(bf16[2880,128]{1,0:T(8,128)(2,1)S(1)} %bitcast.26, f32[64,128]{1,0:T(8,128)S(1)} %get-tuple-element.24.prob_ref, f32[64,128]{1,0:T(8,128)S(1)} %get-tuple-element.25.slot_ref), custom_call_target="tpu_custom_call" | custom-call | tf_op jit(solution)/shard_map/pallas_call | solution.py:517
  50.4 32.1 %all-to-all-done = bf16[64,8,3328]{2,1,0:T(8,128)(2,1)} async-done(((bf16[64,8,3328]{2,1,0:T(8,128)(2,1)}), bf16[64,8,3328]{2,1,0:T(8,128)(2,1)}, u32[]{:S(2)}, u32[]{:S(2)}) %all-to-all-start) | async-done | bytes 3407904 | tf_op jit(solution)/shard_map/all_to_all | solution.py:513
  82.6 5.1 %all-to-all-start.2 = ((bf16[64,8,3328]{2,1,0:T(8,128)(2,1)}), bf16[64,8,3328]{2,1,0:T(8,128)(2,1)S(1)}, u32[]{:S(2)}, u32[]{:S(2)}) async-start(bf16[64,8,3328]{2,1,0:T(8,128)(2,1)} %bitcast.12), calls=%async_computation.2 | async-start | bytes 6815744 | tf_op jit(solution)/shard_map/all_to_all | solution.py:513
  87.7 36.0 %ffn_forward.1 = (bf16[512,3328]{1,0:T(8,128)(2,1)}, f32[576,1536]{1,0:T(8,128)}, f32[576,1536]{1,0:T(8,128)}) custom-call(bf16[512,3328]{1,0:T(8,128)(2,1)} %bitcast.4.x_ref, bf16[2880,1536]{1,0:T(8,128)(2,1)} %decode_gate_up.1.gu_own_ref, bf16[2880,1536]{1,0:T(8,128)(2,1)} %collective-permute-done.gu_oth_ref, bf16[720,2880]{1,0:T(8,128)(2,1)} %decode_down.1.down_own_ref, ...), custom_call_target="tpu_custom_call" | custom-call | tf_op jit(solution)/shard_map/ffn_forward/pallas_call | solution.py:564
  123.7 9.5 %all-to-all-done.2 = bf16[64,8,3328]{2,1,0:T(8,128)(2,1)S(1)} async-done(((bf16[64,8,3328]{2,1,0:T(8,128)(2,1)}), bf16[64,8,3328]{2,1,0:T(8,128)(2,1)S(1)}, u32[]{:S(2)}, u32[]{:S(2)}) %all-to-all-start.2) | async-done | bytes 3407904 | tf_op jit(solution)/shard_map/all_to_all | solution.py:513
  133.2 1.8 copy-done.18
  135.0 5.0 %all-to-all-start.1 = ((bf16[64,8,3328]{2,1,0:T(8,128)(2,1)}), bf16[64,8,3328]{2,1,0:T(8,128)(2,1)S(1)}, u32[]{:S(2)}, u32[]{:S(2)}) async-start(bf16[64,8,3328]{2,1,0:T(8,128)(2,1)} %bitcast.31), calls=%async_computation.1 | async-start | bytes 6815744 | tf_op jit(solution)/shard_map/all_to_all | solution.py:513
  140.0 34.6 %ffn_backward.1 = bf16[512,3328]{1,0:T(8,128)(2,1)} custom-call(bf16[512,3328]{1,0:T(8,128)(2,1)} %bitcast.29, f32[576,1536]{1,0:T(8,128)} %get-tuple-element.30.coef_own_ref, f32[576,1536]{1,0:T(8,128)} %get-tuple-element.31.coef_oth_ref, bf16[720,2880]{1,0:T(8,128)(2,1)} %decode_down.1.down_own_ref, bf16[720,2880]{1,0:T(8,128)(2,1)} %collective-permute-done.1.down_oth_ref, ...), custom_call_target="tpu_custom_call" | custom-call | tf_op jit(solution)/shard_map/ffn_backward/pallas_call | solution.py:589
  174.6 10.3 %all-to-all-done.1 = bf16[64,8,3328]{2,1,0:T(8,128)(2,1)S(1)} async-done(((bf16[64,8,3328]{2,1,0:T(8,128)(2,1)}), bf16[64,8,3328]{2,1,0:T(8,128)(2,1)S(1)}, u32[]{:S(2)}, u32[]{:S(2)}) %all-to-all-start.1) | async-done | bytes 3407904 | tf_op jit(solution)/shard_map/all_to_all | solution.py:513
  184.9 5.8 %all-to-all-start.3 = ((bf16[64,8,3328]{2,1,0:T(8,128)(2,1)}), bf16[64,8,3328]{2,1,0:T(8,128)(2,1)}, u32[]{:S(2)}, u32[]{:S(2)}) async-start(bf16[64,8,3328]{2,1,0:T(8,128)(2,1)} %bitcast.30), calls=%async_computation.3 | async-start | bytes 6815744 | tf_op jit(solution)/shard_map/all_to_all | solution.py:513
  191.9 1.1 copy-done.6
  194.0 4.9 %shard_map.106 = (bf16[2880,128]{1,0:T(8,128)(2,1)}, f32[128,2880]{1,0:T(8,128)S(1)}) custom-call(bf16[512,3328]{1,0:T(8,128)(2,1)S(1)} %bitcast.20, bf16[128,2880]{1,0:T(8,128)(2,1)S(1)} %copy-done.3, bf16[128,2880]{1,0:T(8,128)(2,1)S(1)} %copy-done.6, f32[64,128]{1,0:T(8,128)S(1)} %get-tuple-element.24.prob_ref, f32[64,128]{1,0:T(8,128)S(1)} %get-tuple-element.25.slot_ref, ...), custom_call_target="tpu_custom_call" | custom-call | tf_op jit(solution)/shard_map/pallas_call | solution.py:619
  198.8 1.1 copy-done.8
  200.0 34.1 %all-to-all-done.3 = bf16[64,8,3328]{2,1,0:T(8,128)(2,1)} async-done(((bf16[64,8,3328]{2,1,0:T(8,128)(2,1)}), bf16[64,8,3328]{2,1,0:T(8,128)(2,1)}, u32[]{:S(2)}, u32[]{:S(2)}) %all-to-all-start.3) | async-done | bytes 3407904 | tf_op jit(solution)/shard_map/all_to_all | solution.py:513
  234.1 1.1 copy-done.4
  236.4 1.4 copy-done.9
  238.6 4.5 %shard_map.107 = bf16[2880,128]{1,0:T(8,128)(2,1)} custom-call(bf16[512,3328]{1,0:T(8,128)(2,1)} %bitcast.15.msg_ref, bf16[128,2880]{1,0:T(8,128)(2,1)S(1)} %copy-done.4, bf16[128,2880]{1,0:T(8,128)(2,1)S(1)} %copy-done.7, f32[64,128]{1,0:T(8,128)S(1)} %get-tuple-element.25.slot_ref, bf16[16,2880]{1,0:T(8,128)(2,1)S(1)} %copy-done.16, f32[128,2880]{1,0:T(8,128)S(1)} %copy-done.9), custom_call_target="tpu_custom_call" | custom-call | tf_op jit(solution)/shard_map/pallas_call | solution.py:624
  (39 shorter events, 9.5 us)
Async XLA Ops:
  1.3 1.1 copy-start.10
  2.4 1.0 copy-start.12
  8.8 1.5 copy-start.2
  8.8 1.5 copy-start.13
  10.3 3.5 %copy-start = (s32[1,1440,1440]{2,1,0:T(8,128)S(1)}, s32[1,1440,1440]{2,1,0:T(8,128)}, u32[]{:S(2)}) copy-start(s32[1,1440,1440]{2,1,0:T(8,128)} %param.13) | copy-start | bytes 24883204
  24.4 63.3 %collective-permute-start = (bf16[2880,1536]{1,0:T(8,128)(2,1)}, bf16[2880,1536]{1,0:T(8,128)(2,1)}, u32[]{:S(2)}, u32[]{:S(2)}) collective-permute-start(bf16[2880,1536]{1,0:T(8,128)(2,1)} %decode_gate_up.1.gu_own_ref), channel_id=1, source_target_pairs={{0,1},{1,0},{2,3},{3,2},{4,5},{5,4},{6,7},{7,6},{8,9},{9,8},{10,11... | collective-permute-start | bytes 26542088 | tf_op jit(solution)/shard_map/ppermute | solution.py:552
  24.4 11.9 %copy-start.19 = (s32[1,720,90]{1,0,2:T(1,128)S(1)}, s32[1,720,90]{1,0,2:T(1,128)}, u32[]{:S(2)}) copy-start(s32[1,720,90]{1,0,2:T(1,128)} %param.16) | copy-start | bytes 777604
  24.4 58.2 %all-to-all-start = ((bf16[64,8,3328]{2,1,0:T(8,128)(2,1)}), bf16[64,8,3328]{2,1,0:T(8,128)(2,1)}, u32[]{:S(2)}, u32[]{:S(2)}) async-start(bf16[64,8,3328]{2,1,0:T(8,128)(2,1)} %bitcast.3), calls=%async_computation | async-start | bytes 6815744 | tf_op jit(solution)/shard_map/all_to_all | solution.py:513
  36.5 2.3 copy-start.1
  38.8 7.6 %copy-start.11 = (bf16[128,2880]{0,1:T(8,128)(2,1)S(1)}, bf16[128,2880]{0,1:T(8,128)(2,1)}, u32[]{:S(2)}) copy-start(bf16[128,2880]{0,1:T(8,128)(2,1)} %param.17) | copy-start | bytes 2211844
  46.1 41.5 %collective-permute-start.1 = (bf16[720,2880]{1,0:T(8,128)(2,1)}, bf16[720,2880]{1,0:T(8,128)(2,1)}, u32[]{:S(2)}, u32[]{:S(2)}) collective-permute-start(bf16[720,2880]{1,0:T(8,128)(2,1)} %decode_down.1.down_own_ref), channel_id=1, source_target_pairs={{0,1},{1,0},{2,3},{3,2},{4,5},{5,4},{6,7},{7,6},{8,9},{9,8},{10,11... | collective-permute-start | bytes 12441608 | tf_op jit(solution)/shard_map/ppermute | solution.py:553
  49.6 0.9 copy-start.5
  82.6 50.6 %all-to-all-start.2 = ((bf16[64,8,3328]{2,1,0:T(8,128)(2,1)}), bf16[64,8,3328]{2,1,0:T(8,128)(2,1)S(1)}, u32[]{:S(2)}, u32[]{:S(2)}) async-start(bf16[64,8,3328]{2,1,0:T(8,128)(2,1)} %bitcast.12), calls=%async_computation.2 | async-start | bytes 6815744 | tf_op jit(solution)/shard_map/all_to_all | solution.py:513
  133.2 1.8 copy-start.18
  135.0 50.0 %all-to-all-start.1 = ((bf16[64,8,3328]{2,1,0:T(8,128)(2,1)}), bf16[64,8,3328]{2,1,0:T(8,128)(2,1)S(1)}, u32[]{:S(2)}, u32[]{:S(2)}) async-start(bf16[64,8,3328]{2,1,0:T(8,128)(2,1)} %bitcast.31), calls=%async_computation.1 | async-start | bytes 6815744 | tf_op jit(solution)/shard_map/all_to_all | solution.py:513
  184.9 49.2 %all-to-all-start.3 = ((bf16[64,8,3328]{2,1,0:T(8,128)(2,1)}), bf16[64,8,3328]{2,1,0:T(8,128)(2,1)}, u32[]{:S(2)}, u32[]{:S(2)}) async-start(bf16[64,8,3328]{2,1,0:T(8,128)(2,1)} %bitcast.30), calls=%async_computation.3 | async-start | bytes 6815744 | tf_op jit(solution)/shard_map/all_to_all | solution.py:513
  190.7 1.1 copy-start.3
  191.9 1.1 copy-start.6
  193.0 1.0 copy-start.14
  198.8 1.1 copy-start.8
  234.1 1.1 copy-start.4
  235.2 1.1 copy-start.7
  236.4 1.4 copy-start.9
  237.7 0.9 copy-start.16
  (2 other events, 1.3 us)

commit v2 on v1

--- a/solution.py
+++ b/solution.py
@@ -92,6 +92,22 @@
             fold_sc[j, pl.ds(r, experts, stride=SLOTS), :] = nine[:, at : at + LANE]
         at = tail_at + j * LANE
         msg_ref[:, at : at + LANE] = fold_sc[j].astype(BF16)
+
+
+def fetch(msg_ref, main_sc, tail_sc, sem, tail_at):
+    rows = msg_ref.shape[0]
+    pair = (
+        pltpu.make_async_copy(
+            msg_ref.at[:, pl.ds(0, tail_at)], main_sc.at[pl.ds(0, rows), pl.ds(0, tail_at)], sem.at[0]
+        ),
+        pltpu.make_async_copy(
+            msg_ref.at[:, pl.ds(tail_at, tail_sc.shape[1])], tail_sc, sem.at[1]
+        ),
+    )
+    for copy in pair:
+        copy.start()
+    for copy in pair:
+        copy.wait()
 
 
 def get_tail(msg_ref, fold_sc, put, tail_at, tail, experts):
@@ -112,7 +128,7 @@
     experts = router_ref.shape[0]
     tail_at, tail = tail_geometry(width)
     order_rows(tok_ref, tokp_ref)
-    gain_sc[...] = jnp.broadcast_to(gain_ref[...], gain_sc.shape)
+    gain_sc[...] = jnp.broadcast_to(gain_ref[...].reshape(1, width), gain_sc.shape)
     order_columns(gain_sc, gainp_ref)
     order_columns(router_ref, routerp_ref)
     tok = tokp_ref[...].astype(F32)
@@ -230,7 +246,7 @@
 def ffn_forward_kernel(
     x_ref, gu_own_ref, gu_oth_ref, down_own_ref, down_oth_ref,
     out_ref, coef_own_ref, coef_oth_ref,
-    x_sc, pre_sc, act_own_sc, act_oth_sc, res_sc, fold_sc,
+    x_sc, pre_sc, act_own_sc, act_oth_sc, res_sc, fold_sc, tail_sc, sem,
     *, width, half, n_up, n_down,
 ):
     step = pl.program_id(0)
@@ -244,12 +260,12 @@
 
     @pl.when(step == 0)
     def _():
-        x_sc[:rows, :width] = x_ref[:, :width]
+        fetch(x_ref, x_sc, tail_sc, sem, tail_at)
 
         def put(at, value):
             x_sc[rows:, at : at + LANE] = value
 
-        get_tail(x_ref, fold_sc, put, tail_at, tail, experts)
+        get_tail(tail_sc, fold_sc, put, 0, tail, experts)
 
     def up(gu_ref, index):
         at = pl.multiple_of(index * tile_up, tile_up)
@@ -322,7 +338,7 @@
 def ffn_backward_kernel(
     g_ref, coef_own_ref, coef_oth_ref, down_own_ref, down_oth_ref, gu_own_ref, gu_oth_ref,
     out_ref,
-    g_sc, back_sc, pre_own_sc, pre_oth_sc, res_sc, fold_sc,
+    g_sc, back_sc, pre_own_sc, pre_oth_sc, res_sc, fold_sc, tail_sc, sem,
     *, width, half, inner, n_back,
 ):
     step = pl.program_id(0)
@@ -335,12 +351,12 @@
 
     @pl.when(step == 0)
     def _():
-        g_sc[:rows, :width] = g_ref[:, :width]
+        fetch(g_ref, g_sc, tail_sc, sem, tail_at)
 
         def put(at, value):
             g_sc[rows:, at : at + LANE] = value
 
-        get_tail(g_ref, fold_sc, put, tail_at, tail, experts)
+        get_tail(tail_sc, fold_sc, put, 0, tail, experts)
 
     def finish(coef_ref, pre_sc):
         chunk = 16
@@ -423,35 +439,60 @@
 def combine_back_kernel(
     msg_ref, tokp_ref, cotp_ref, slot_ref, gain_ref, dnormed_ref,
     grad_ref,
-    nine_sc, fold_sc, sum_sc,
+    nine_sc, fold_sc, sum_sc, msg_sc, tok_sc, cot_sc, dn_sc, sem,
 ):
     toks, width = tokp_ref.shape
     experts = slot_ref.shape[0]
     tail_at, tail = tail_geometry(width)
-
-    def put(at, value):
-        nine_sc[:, at : at + LANE] = value
-
-    get_tail(msg_ref, fold_sc, put, tail_at, tail, experts)
+    step = 4 * PAIR
+    pieces = [(at, min(step, tail_at - at)) for at in range(0, tail_at, step)]
+    pieces = [(tail_at, tail)] + pieces
+    singles = [
+        pltpu.make_async_copy(src, dst, sem.at[i])
+        for i, (src, dst) in enumerate(((tokp_ref, tok_sc), (dnormed_ref, dn_sc), (cotp_ref, cot_sc)))
+    ]
+    chunks = [
+        pltpu.make_async_copy(
+            msg_ref.at[:, pl.ds(at, size)], msg_sc.at[:, pl.ds(at, size)], sem.at[len(singles) + i]
+        )
+        for i, (at, size) in enumerate(pieces)
+    ]
+    for copy in singles + chunks:
+        copy.start()
     hot, hot_nine = slot_hot(slot_ref[...])
     pick = jnp.concatenate([hot, hot_nine], axis=0).T.astype(BF16)
     main = experts * SLOTS
-    tok = tokp_ref[...].astype(F32)
-    inv = lax.rsqrt(jnp.sum(tok * tok, axis=1, keepdims=True) / width + norm_epsilon)
+    for copy in singles:
+        copy.wait()
+    square = jnp.zeros((toks, 1), F32)
+    for start in range(0, width, 2 * PAIR):
+        tok = tok_sc[:, start : min(start + 2 * PAIR, width)].astype(F32)
+        square = square + jnp.sum(tok * tok, axis=1, keepdims=True)
+    inv = lax.rsqrt(square / width + norm_epsilon)
+    chunks[0].wait()
+
+    def put(at, value):
+        nine_sc[:, at : at + LANE] = value
+
+    get_tail(msg_sc, fold_sc, put, tail_at, tail, experts)
     along = jnp.zeros((toks, 1), F32)
-    for start in range(0, width, 2 * PAIR):
-        stop = min(start + 2 * PAIR, width)
-        total = mm(pick[:, :main], msg_ref[:, start:stop]) + mm(pick[:, main:], nine_sc[:, start:stop])
-        total = (total + dnormed_ref[:, start:stop]) * gain_ref[0:1, start:stop].astype(F32)
-        sum_sc[:, start:stop] = total
-        along = along + jnp.sum(total * tokp_ref[:, start:stop].astype(F32), axis=1, keepdims=True)
+    for copy, (at, size) in zip(chunks[1:], pieces[1:]):
+        copy.wait()
+        for start in range(at, min(at + size, width), 2 * PAIR):
+            stop = min(start + 2 * PAIR, at + size, width)
+            total = mm(pick[:, :main], msg_sc[:, start:stop]) + mm(
+                pick[:, main:], nine_sc[:, start:stop]
+            )
+            total = (total + dn_sc[:, start:stop]) * gain_ref[0:1, start:stop].astype(F32)
+            sum_sc[:, start:stop] = total
+            along = along + jnp.sum(total * tok_sc[:, start:stop].astype(F32), axis=1, keepdims=True)
     cube = inv * inv * inv * (along / width)
 
     def load(start, size):
         value = (
-            cotp_ref[:, start : start + size].astype(F32)
+            cot_sc[:, start : start + size].astype(F32)
             + inv * sum_sc[:, start : start + size]
-            - tokp_ref[:, start : start + size].astype(F32) * cube
+            - tok_sc[:, start : start + size].astype(F32) * cube
         )
         return value.astype(BF16)
 
@@ -468,7 +509,7 @@
 
 def simple_call(kernel, outs, scratch):
     return pl.pallas_call(
-        kernel, out_shape=outs, scratch_shapes=scratch, compiler_params=params(24)
+        kernel, out_shape=outs, scratch_shapes=scratch, compiler_params=params(63)
     )
 
 
@@ -490,7 +531,6 @@
     all_rows = rows + experts
     wide = SLOTS * tail
     padded = up_to(inner, PAIR)
-    gain = norm_gain.reshape(1, width)
 
     nine_f = pltpu.VMEM((experts, wide), F32)
     nine_b = pltpu.VMEM((experts, wide), BF16)
@@ -503,7 +543,7 @@
         dispatch_rows_kernel,
         (msg, table, table, block, struct((16, width), BF16), struct((experts, width), BF16)),
         [pltpu.VMEM((toks, width), BF16), pltpu.VMEM((16, width), BF16), nine_f, fold],
-    )(tokens.T, gain, router_weight.T, expert_ids.T)
+    )(tokens.T, norm_gain, router_weight.T, expert_ids.T)
     row_msg, gate_up_words, down_words = lax.optimization_barrier(
         (row_msg, gate_up_words, down_words)
     )
@@ -531,7 +571,7 @@
         ],
         out_specs=pl.BlockSpec((PAIR, padded), lambda i: (i, 0)),
         scratch_shapes=[pltpu.VMEM((LANE // group_rows, inner), F32)],
-        compiler_params=params(24),
+        compiler_params=params(63),
         name="decode_gate_up",
     )(gate_up_words[0], gate_up_scales[0])
     down_rows = 144
@@ -545,7 +585,7 @@
         ],
         out_specs=pl.BlockSpec((down_rows, 2 * word_cols), lambda i: (i, 0)),
         scratch_shapes=[pltpu.VMEM((down_rows, word_cols), F32)],
-        compiler_params=params(24),
+        compiler_params=params(63),
         name="decode_down",
     )(down_words[0], down_scales[0])
     swap = [(0, 1), (1, 0)]
@@ -566,7 +606,7 @@
         out_shape=(msg, coef, coef),
         grid=(2 * n_up + n_down,),
         in_specs=[
-            once((rows, msg_width)),
+            pl.BlockSpec(memory_space=pltpu.HBM),
             pl.BlockSpec((width, tile), lambda i: (0, clip(i, 0, n_up))),
             pl.BlockSpec((width, tile), lambda i: (0, clip(i, n_up, n_up))),
             pl.BlockSpec((half, tile), lambda i: (0, clip(i, 2 * n_up, n_down))),
@@ -580,8 +620,10 @@
             pltpu.VMEM((all_rows, half_wide), BF16),
             pltpu.VMEM((all_rows, n_down * tile), F32),
             fold,
+            pltpu.VMEM((rows, tail), BF16),
+            pltpu.SemaphoreType.DMA((2,)),
         ],
-        compiler_params=params(52),
+        compiler_params=params(63),
         name="ffn_forward",
     )(rows_in, gate_up, gate_up_other, down, down_other)
     outs_in = exchange(out_msg)
@@ -593,7 +635,7 @@
         out_shape=msg,
         grid=(2 + n_down,),
         in_specs=[
-            once((rows, msg_width)),
+            pl.BlockSpec(memory_space=pltpu.HBM),
             once((all_rows, padded)),
             once((all_rows, padded)),
             once((half, width)),
@@ -609,8 +651,10 @@
             pltpu.VMEM((all_rows, padded), BF16),
             pltpu.VMEM((all_rows, n_down * tile), F32),
             fold,
+            pltpu.VMEM((rows, tail), BF16),
+            pltpu.SemaphoreType.DMA((2,)),
         ],
-        compiler_params=params(52),
+        compiler_params=params(63),
         name="ffn_backward",
     )(grads_in, coef_own, coef_oth, down, down_other, gate_up, gate_up_other)
     backs_in = exchange(back_msg)
@@ -621,8 +665,23 @@
         (turned, struct((toks, width), F32)),
         [nine_b, fold, pltpu.VMEM((toks, width), BF16)],
     )(outs_in, tokp, cotp, prob, slot, routerp)
-    token_grad = simple_call(
-        combine_back_kernel, turned, [nine_b, fold, pltpu.VMEM((toks, width), F32)]
+    in_hbm, in_vmem = pl.BlockSpec(memory_space=pltpu.HBM), pl.BlockSpec(memory_space=pltpu.VMEM)
+    token_grad = pl.pallas_call(
+        combine_back_kernel,
+        out_shape=turned,
+        in_specs=[in_hbm, in_hbm, in_hbm, in_vmem, in_vmem, in_hbm],
+        scratch_shapes=[
+            nine_b,
+            fold,
+            pltpu.VMEM((toks, width), F32),
+            pltpu.VMEM((rows, msg_width), BF16),
+            pltpu.VMEM((toks, width), BF16),
+            pltpu.VMEM((toks, width), BF16),
+            pltpu.VMEM((toks, width), F32),
+            pltpu.SemaphoreType.DMA((4 + -(-tail_at // (4 * PAIR)),)),
+        ],
+        compiler_params=params(63),
+        name="combine_back",
     )(backs_in, tokp, cotp, slot, gainp, dnormed)
     return mixed.T, token_grad.T
 

time: 244 us -> 238 us (0.975)
  local copies, waits for them, and re-layouts: 23 us -> 2.85 us
  Pallas kernels: 105 us -> 120 us
    unnamed x42 -> x4, local copies, waits for them, and re-layouts: 22.3 us -> 2.85 us
    pallas_call x1, Pallas kernels: 10.5 us -> 14.5 us  [shards(): pl.pallas_call(functools.partial(decode_rows_kernel, word_rows - (steps -...]
    pallas_call x1, Pallas kernels: 4.86 us -> 8.52 us  [shards(): simple_call(combine_out_kernel, (turned, struct((toks, width), F32)), [ni...]
  transfers between devices with their start and end apart: 6 -> 6, of which waited for: 4 -> 4; matrix products, arithmetic and copies ran while one was open for 0% -> 0% of each run, Pallas kernels for 35% -> 40%
where the time goes in v2:
time: 238 us; the launch traced here: 237 us
  Pallas kernels  120 us (50%)
  waiting for transfers between devices  84.1 us (35%)
  starting transfers between devices  29.1 us (12%)
  local copies, waits for them, and re-layouts  2.85 us (1%)
    all_to_all x4, waiting for transfers between devices, exchange(): swapped = lax.all_to_all(shaped, ('dp', 'x'), 0, 0, tiled=True)  84.1 us
    pallas_call x1, Pallas kernels, shards(): pl.pallas_call(functools.partial(ffn_forward_kernel, width=width, half=ha...  36.9 us
    pallas_call x1, Pallas kernels, shards(): pl.pallas_call(functools.partial(ffn_backward_kernel, width=width, half=h...  35.5 us
    all_to_all x4, starting transfers between devices, exchange(): swapped = lax.all_to_all(shaped, ('dp', 'x'), 0, 0, tiled=True)  28.9 us
    pallas_call x1, Pallas kernels, shards(): pl.pallas_call(functools.partial(decode_rows_kernel, word_rows - (steps -...  14.5 us
    pallas_call x1, Pallas kernels, shards(): pl.pallas_call(decode_cols_kernel, out_shape=struct((half, 2 * word_cols)...  8.87 us
    pallas_call x1, Pallas kernels, shards(): simple_call(combine_out_kernel, (turned, struct((toks, width), F32)), [ni...  8.52 us
    pallas_call x1, Pallas kernels, shards(): pl.pallas_call(combine_back_kernel, out_shape=turned, in_specs=[in_hbm, i...  6.01 us
  transfers between devices with their start and end apart: 6, of which 4 were waited for; matrix products, arithmetic and copies ran while one was open for 0% of the time, Pallas kernels for 40%

profile of v2, /device:TPU:0, one launch (start us, length us, event | category | flops | bytes accessed | tf_op | source)
XLA Modules:
  0.0 236.8 jit_solution(4784541907708912329)
XLA Ops:
  0.6 5.3 %shard_map.104 = (bf16[512,3328]{1,0:T(8,128)(2,1)}, f32[64,128]{1,0:T(8,128)}, f32[64,128]{1,0:T(8,128)}, bf16[128,2880]{1,0:T(8,128)(2,1)}, bf16[16,2880]{1,0:T(8,128)(2,1)}, /*index=5*/bf16[64,2880]{1,0:T(8,128)(2,1)}) custom-call(bf16[2880,128]{1,0:T(8,128)(2,1)} %bitcast.29, bf16[2880]{0:T(1024)(128)(2,1)} %gain_ref.1, bf16[64,2880]{1,0:T(8,128)(2,1)} %bitcast.31, ...), custom_call_target="tpu_custom_call" | custom-call | tf_op jit(solution)/shard_map/pallas_call | solution.py:542
  5.9 1.9 copy.14
  7.8 14.5 %decode_gate_up.1.gu_own_ref = bf16[2880,1536]{1,0:T(8,128)(2,1)} custom-call(s32[1440,1440]{1,0:T(8,128)} %bitcast.21, s32[90,1440]{1,0:T(8,128)} %bitcast.26), custom_call_target="tpu_custom_call" | custom-call | tf_op jit(solution)/shard_map/decode_gate_up/pallas_call | solution.py:564
  22.3 0.0 collective-permute-start
  22.3 0.0 copy-start
  22.3 11.9 %all-to-all-start = ((bf16[64,8,3328]{2,1,0:T(8,128)(2,1)}), bf16[64,8,3328]{2,1,0:T(8,128)(2,1)}, u32[]{:S(2)}, u32[]{:S(2)}) async-start(bf16[64,8,3328]{2,1,0:T(8,128)(2,1)} %bitcast.23), calls=%async_computation | async-start | bytes 6815744 | tf_op jit(solution)/shard_map/all_to_all | solution.py:553
  34.2 0.0 copy-done
  34.2 0.9 copy.11
  35.1 8.9 %decode_down.1.down_own_ref = bf16[720,2880]{1,0:T(8,128)(2,1)} custom-call(s32[720,1440]{1,0:T(8,128)} %bitcast.22, s32[720,90]{1,0:T(8,128)} %bitcast.27), custom_call_target="tpu_custom_call" | custom-call | tf_op jit(solution)/shard_map/decode_down/pallas_call | solution.py:578
  44.0 0.2 collective-permute-start.1
  44.2 4.3 %shard_map.105 = (bf16[512,3328]{1,0:T(8,128)(2,1)}, bf16[128,2880]{1,0:T(8,128)(2,1)}) custom-call(bf16[2880,128]{1,0:T(8,128)(2,1)} %bitcast.28, f32[64,128]{1,0:T(8,128)} %get-tuple-element.24.prob_ref, f32[64,128]{1,0:T(8,128)} %get-tuple-element.25.slot_ref), custom_call_target="tpu_custom_call" | custom-call | tf_op jit(solution)/shard_map/pallas_call | solution.py:557
  48.5 31.9 %all-to-all-done = bf16[64,8,3328]{2,1,0:T(8,128)(2,1)} async-done(((bf16[64,8,3328]{2,1,0:T(8,128)(2,1)}), bf16[64,8,3328]{2,1,0:T(8,128)(2,1)}, u32[]{:S(2)}, u32[]{:S(2)}) %all-to-all-start) | async-done | bytes 3407904 | tf_op jit(solution)/shard_map/all_to_all | solution.py:553
  80.5 5.6 %all-to-all-start.2 = ((bf16[64,8,3328]{2,1,0:T(8,128)(2,1)}), bf16[64,8,3328]{2,1,0:T(8,128)(2,1)}, u32[]{:S(2)}, u32[]{:S(2)}) async-start(bf16[64,8,3328]{2,1,0:T(8,128)(2,1)} %bitcast.24), calls=%async_computation.2 | async-start | bytes 6815744 | tf_op jit(solution)/shard_map/all_to_all | solution.py:553
  86.0 0.0 collective-permute-done.1.down_oth_ref
  86.1 0.0 collective-permute-done.gu_oth_ref
  86.1 36.9 %ffn_forward.1 = (bf16[512,3328]{1,0:T(8,128)(2,1)}, f32[576,1536]{1,0:T(8,128)}, f32[576,1536]{1,0:T(8,128)}) custom-call(bf16[512,3328]{1,0:T(8,128)(2,1)} %bitcast.4.x_ref, bf16[2880,1536]{1,0:T(8,128)(2,1)} %decode_gate_up.1.gu_own_ref, bf16[2880,1536]{1,0:T(8,128)(2,1)} %collective-permute-done.gu_oth_ref, bf16[720,2880]{1,0:T(8,128)(2,1)} %decode_down.1.down_own_ref, ...), custom_call_target="tpu_custom_call" | custom-call | tf_op jit(solution)/shard_map/ffn_forward/pallas_call | solution.py:604
  122.9 8.0 %all-to-all-done.2 = bf16[64,8,3328]{2,1,0:T(8,128)(2,1)} async-done(((bf16[64,8,3328]{2,1,0:T(8,128)(2,1)}), bf16[64,8,3328]{2,1,0:T(8,128)(2,1)}, u32[]{:S(2)}, u32[]{:S(2)}) %all-to-all-start.2) | async-done | bytes 3407904 | tf_op jit(solution)/shard_map/all_to_all | solution.py:553
  130.9 5.8 %all-to-all-start.1 = ((bf16[64,8,3328]{2,1,0:T(8,128)(2,1)}), bf16[64,8,3328]{2,1,0:T(8,128)(2,1)}, u32[]{:S(2)}, u32[]{:S(2)}) async-start(bf16[64,8,3328]{2,1,0:T(8,128)(2,1)} %bitcast.25), calls=%async_computation.1 | async-start | bytes 6815744 | tf_op jit(solution)/shard_map/all_to_all | solution.py:553
  136.7 35.5 %ffn_backward.1 = bf16[512,3328]{1,0:T(8,128)(2,1)} custom-call(bf16[512,3328]{1,0:T(8,128)(2,1)} %bitcast.13.g_ref, f32[576,1536]{1,0:T(8,128)} %get-tuple-element.30.coef_own_ref, f32[576,1536]{1,0:T(8,128)} %get-tuple-element.31.coef_oth_ref, bf16[720,2880]{1,0:T(8,128)(2,1)} %decode_down.1.down_own_ref, ...), custom_call_target="tpu_custom_call" | custom-call | tf_op jit(solution)/shard_map/ffn_backward/pallas_call | solution.py:631
  172.2 9.5 %all-to-all-done.1 = bf16[64,8,3328]{2,1,0:T(8,128)(2,1)} async-done(((bf16[64,8,3328]{2,1,0:T(8,128)(2,1)}), bf16[64,8,3328]{2,1,0:T(8,128)(2,1)}, u32[]{:S(2)}, u32[]{:S(2)}) %all-to-all-start.1) | async-done | bytes 3407904 | tf_op jit(solution)/shard_map/all_to_all | solution.py:553
  181.7 5.6 %all-to-all-start.3 = ((bf16[64,8,3328]{2,1,0:T(8,128)(2,1)}), bf16[64,8,3328]{2,1,0:T(8,128)(2,1)}, u32[]{:S(2)}, u32[]{:S(2)}) async-start(bf16[64,8,3328]{2,1,0:T(8,128)(2,1)} %bitcast.20), calls=%async_computation.3 | async-start | bytes 6815744 | tf_op jit(solution)/shard_map/all_to_all | solution.py:553
  187.3 8.5 %shard_map.106 = (bf16[2880,128]{1,0:T(8,128)(2,1)}, f32[128,2880]{1,0:T(8,128)}) custom-call(bf16[512,3328]{1,0:T(8,128)(2,1)} %bitcast.9.msg_ref, bf16[128,2880]{1,0:T(8,128)(2,1)} %get-tuple-element.23.tokp_ref, bf16[128,2880]{1,0:T(8,128)(2,1)} %get-tuple-element.26.cotp_ref, f32[64,128]{1,0:T(8,128)} %get-tuple-element.24.prob_ref, ...), custom_call_target="tpu_custom_call" | custom-call | tf_op jit(solution)/shard_map/pallas_call | solution.py:663
  195.9 34.7 %all-to-all-done.3 = bf16[64,8,3328]{2,1,0:T(8,128)(2,1)} async-done(((bf16[64,8,3328]{2,1,0:T(8,128)(2,1)}), bf16[64,8,3328]{2,1,0:T(8,128)(2,1)}, u32[]{:S(2)}, u32[]{:S(2)}) %all-to-all-start.3) | async-done | bytes 3407904 | tf_op jit(solution)/shard_map/all_to_all | solution.py:553
  230.6 6.0 %combine_back.1 = bf16[2880,128]{1,0:T(8,128)(2,1)} custom-call(bf16[512,3328]{1,0:T(8,128)(2,1)} %bitcast.15.msg_ref, bf16[128,2880]{1,0:T(8,128)(2,1)} %get-tuple-element.23.tokp_ref, bf16[128,2880]{1,0:T(8,128)(2,1)} %get-tuple-element.26.cotp_ref, f32[64,128]{1,0:T(8,128)} %get-tuple-element.25.slot_ref, bf16[16,2880]{1,0:T(8,128)(2,1)} %get-tuple-element.32.gain_ref, ...), custom_call_target="tpu_custom_call" | custom-call | tf_op jit(solution)/shard_map/combine_back/pallas_call | solution.py:669
Async XLA Ops:
  22.3 63.8 %collective-permute-start = (bf16[2880,1536]{1,0:T(8,128)(2,1)}, bf16[2880,1536]{1,0:T(8,128)(2,1)}, u32[]{:S(2)}, u32[]{:S(2)}) collective-permute-start(bf16[2880,1536]{1,0:T(8,128)(2,1)} %decode_gate_up.1.gu_own_ref), channel_id=1, source_target_pairs={{0,1},{1,0},{2,3},{3,2},{4,5},{5,4},{6,7},{7,6},{8,9},{9,8},{10,11... | collective-permute-start | bytes 26542088 | tf_op jit(solution)/shard_map/ppermute | solution.py:592
  22.3 11.9 %copy-start = (s32[1,720,90]{1,0,2:T(1,128)S(1)}, s32[1,720,90]{1,0,2:T(1,128)}, u32[]{:S(2)}) copy-start(s32[1,720,90]{1,0,2:T(1,128)} %param.16) | copy-start | bytes 777604
  22.3 58.2 %all-to-all-start = ((bf16[64,8,3328]{2,1,0:T(8,128)(2,1)}), bf16[64,8,3328]{2,1,0:T(8,128)(2,1)}, u32[]{:S(2)}, u32[]{:S(2)}) async-start(bf16[64,8,3328]{2,1,0:T(8,128)(2,1)} %bitcast.23), calls=%async_computation | async-start | bytes 6815744 | tf_op jit(solution)/shard_map/all_to_all | solution.py:553
  44.0 42.0 %collective-permute-start.1 = (bf16[720,2880]{1,0:T(8,128)(2,1)}, bf16[720,2880]{1,0:T(8,128)(2,1)}, u32[]{:S(2)}, u32[]{:S(2)}) collective-permute-start(bf16[720,2880]{1,0:T(8,128)(2,1)} %decode_down.1.down_own_ref), channel_id=1, source_target_pairs={{0,1},{1,0},{2,3},{3,2},{4,5},{5,4},{6,7},{7,6},{8,9},{9,8},{10,11... | collective-permute-start | bytes 12441608 | tf_op jit(solution)/shard_map/ppermute | solution.py:593
  80.5 50.5 %all-to-all-start.2 = ((bf16[64,8,3328]{2,1,0:T(8,128)(2,1)}), bf16[64,8,3328]{2,1,0:T(8,128)(2,1)}, u32[]{:S(2)}, u32[]{:S(2)}) async-start(bf16[64,8,3328]{2,1,0:T(8,128)(2,1)} %bitcast.24), calls=%async_computation.2 | async-start | bytes 6815744 | tf_op jit(solution)/shard_map/all_to_all | solution.py:553
  130.9 50.8 %all-to-all-start.1 = ((bf16[64,8,3328]{2,1,0:T(8,128)(2,1)}), bf16[64,8,3328]{2,1,0:T(8,128)(2,1)}, u32[]{:S(2)}, u32[]{:S(2)}) async-start(bf16[64,8,3328]{2,1,0:T(8,128)(2,1)} %bitcast.25), calls=%async_computation.1 | async-start | bytes 6815744 | tf_op jit(solution)/shard_map/all_to_all | solution.py:553
  181.7 48.9 %all-to-all-start.3 = ((bf16[64,8,3328]{2,1,0:T(8,128)(2,1)}), bf16[64,8,3328]{2,1,0:T(8,128)(2,1)}, u32[]{:S(2)}, u32[]{:S(2)}) async-start(bf16[64,8,3328]{2,1,0:T(8,128)(2,1)} %bitcast.20), calls=%async_computation.3 | async-start | bytes 6815744 | tf_op jit(solution)/shard_map/all_to_all | solution.py:553

commit v3 on v2

--- a/solution.py
+++ b/solution.py
@@ -118,29 +118,37 @@
             put(r * tail + j * LANE, fold_sc[j, pl.ds(r, experts, stride=SLOTS), :].astype(BF16))
 
 
+def inverse_rms(tok_ref):
+    toks, width = tok_ref.shape
+    square = jnp.zeros((toks, 1), F32)
+    for start in range(0, width, 4 * PAIR):
+        tok = tok_ref[:, start : min(start + 4 * PAIR, width)].astype(F32)
+        square = square + jnp.sum(tok * tok, axis=1, keepdims=True)
+    return lax.rsqrt(square / width + norm_epsilon)
+
+
+def normalize(tokp_ref, gainp_ref, normp_sc):
+    inv = inverse_rms(tokp_ref)
+    normp_sc[...] = (tokp_ref[...].astype(F32) * inv * gainp_ref[0:1, :].astype(F32)).astype(BF16)
+
+
 def dispatch_rows_kernel(
-    tok_ref, gain_ref, router_ref, ids_ref,
-    msg_ref, prob_ref, slot_ref, tokp_ref, gainp_ref, routerp_ref,
+    tok_ref, gain_ref, ids_ref,
+    msg_ref, slot_ref, tokp_ref, gainp_ref,
     normp_sc, gain_sc, nine_sc, fold_sc,
 ):
     width, toks = tok_ref.shape
     top = ids_ref.shape[0]
-    experts = router_ref.shape[0]
+    experts = slot_ref.shape[0]
     tail_at, tail = tail_geometry(width)
     order_rows(tok_ref, tokp_ref)
     gain_sc[...] = jnp.broadcast_to(gain_ref[...].reshape(1, width), gain_sc.shape)
     order_columns(gain_sc, gainp_ref)
-    order_columns(router_ref, routerp_ref)
-    tok = tokp_ref[...].astype(F32)
-    inv = lax.rsqrt(jnp.sum(tok * tok, axis=1, keepdims=True) / width + norm_epsilon)
-    normp_sc[...] = (tok * inv * gainp_ref[0:1, :].astype(F32)).astype(BF16)
-    logits = mm_nt(routerp_ref[...], normp_sc[...])
+    normalize(tokp_ref, gainp_ref, normp_sc)
     e_idx = iota((experts, toks), 0)
     chosen = e_idx == ids_ref[0:1, :]
     for k in range(1, top):
         chosen = chosen | (e_idx == ids_ref[k : k + 1, :])
-    raised = jnp.where(chosen, jnp.exp(logits), 0.0)
-    prob_ref[...] = raised / jnp.sum(raised, axis=0, keepdims=True)
     earlier = (iota((toks, toks), 0) < iota((toks, toks), 1)).astype(F32).astype(BF16)
     rank = mm(chosen.astype(F32).astype(BF16), earlier)
     slot = jnp.where(chosen, rank, -1.0)
@@ -156,16 +164,22 @@
 
 
 def dispatch_grads_kernel(
-    cot_ref, prob_ref, slot_ref,
-    msg_ref, cotp_ref,
-    nine_sc, fold_sc,
+    cot_ref, slot_ref, tokp_ref, gainp_ref, router_ref,
+    msg_ref, cotp_ref, prob_ref, routerp_ref,
+    normp_sc, nine_sc, fold_sc,
 ):
     width, toks = cot_ref.shape
-    experts = prob_ref.shape[0]
+    experts = slot_ref.shape[0]
     tail_at, tail = tail_geometry(width)
+    order_columns(router_ref, routerp_ref)
+    normalize(tokp_ref, gainp_ref, normp_sc)
+    logits = mm_nt(routerp_ref[...], normp_sc[...])
+    slot = slot_ref[...]
+    raised = jnp.where(slot >= 0.0, jnp.exp(logits), 0.0)
+    prob = raised / jnp.sum(raised, axis=0, keepdims=True)
+    prob_ref[...] = prob
     order_rows(cot_ref, cotp_ref)
-    prob = prob_ref[...]
-    hot, hot_nine = slot_hot(slot_ref[...])
+    hot, hot_nine = slot_hot(slot)
     spread = jnp.broadcast_to(prob[:, None, :], (experts, SLOTS, toks)).reshape(experts * SLOTS, toks)
     row_prob = jnp.sum(hot * spread, axis=1, keepdims=True)
     nine_prob = jnp.sum(hot_nine * prob, axis=1, keepdims=True)
@@ -394,8 +408,8 @@
 
 
 def combine_out_kernel(
-    msg_ref, tokp_ref, cotp_ref, prob_ref, slot_ref, router_ref,
-    mixed_ref, dnormed_ref,
+    msg_ref, tokp_ref, cotp_ref, prob_ref, slot_ref, router_ref, gain_ref,
+    mixed_ref, base_ref, pick_ref, inv_ref,
     nine_sc, fold_sc, mix_sc,
 ):
     toks, width = tokp_ref.shape
@@ -433,64 +447,65 @@
     second = left.astype(BF16)
     third = (left - second.astype(F32)).astype(BF16)
     router = router_ref[...]
-    dnormed_ref[...] = mm(first, router) + mm(second, router) + mm(third, router)
+    dnormed = mm(first, router) + mm(second, router) + mm(third, router)
+    base_ref[...] = dnormed * gain_ref[0:1, :].astype(F32)
+    inv = inverse_rms(tokp_ref)
+    along = jnp.sum(base_ref[...] * tokp_ref[...].astype(F32), axis=1, keepdims=True)
+    cube = inv * inv * inv * (along / width)
+    base_ref[...] = (
+        cotp_ref[...].astype(F32) + inv * base_ref[...] - tokp_ref[...].astype(F32) * cube
+    )
+    inv_ref[...] = jnp.broadcast_to(inv, inv_ref.shape)
+    pick_ref[...] = jnp.concatenate([hot, hot_nine], axis=0).T.astype(BF16)
 
 
 def combine_back_kernel(
-    msg_ref, tokp_ref, cotp_ref, slot_ref, gain_ref, dnormed_ref,
+    msg_ref, tokp_ref, base_ref, pick_ref, inv_ref, gain_ref,
     grad_ref,
-    nine_sc, fold_sc, sum_sc, msg_sc, tok_sc, cot_sc, dn_sc, sem,
+    nine_sc, fold_sc, sum_sc, msg_sc, tok_sc, base_sc, sem,
 ):
     toks, width = tokp_ref.shape
-    experts = slot_ref.shape[0]
+    experts = nine_sc.shape[0]
+    main = experts * SLOTS
     tail_at, tail = tail_geometry(width)
     step = 4 * PAIR
-    pieces = [(at, min(step, tail_at - at)) for at in range(0, tail_at, step)]
-    pieces = [(tail_at, tail)] + pieces
-    singles = [
-        pltpu.make_async_copy(src, dst, sem.at[i])
-        for i, (src, dst) in enumerate(((tokp_ref, tok_sc), (dnormed_ref, dn_sc), (cotp_ref, cot_sc)))
-    ]
+    pieces = [(tail_at, tail)] + [(at, min(step, tail_at - at)) for at in range(0, tail_at, step)]
     chunks = [
         pltpu.make_async_copy(
-            msg_ref.at[:, pl.ds(at, size)], msg_sc.at[:, pl.ds(at, size)], sem.at[len(singles) + i]
+            msg_ref.at[:, pl.ds(at, size)], msg_sc.at[:, pl.ds(at, size)], sem.at[2 + i]
         )
         for i, (at, size) in enumerate(pieces)
     ]
-    for copy in singles + chunks:
+    tok_copy = pltpu.make_async_copy(tokp_ref, tok_sc, sem.at[0])
+    base_copy = pltpu.make_async_copy(base_ref, base_sc, sem.at[1])
+    copies = [chunks[0], tok_copy] + chunks[1:] + [base_copy]
+    for copy in copies:
         copy.start()
-    hot, hot_nine = slot_hot(slot_ref[...])
-    pick = jnp.concatenate([hot, hot_nine], axis=0).T.astype(BF16)
-    main = experts * SLOTS
-    for copy in singles:
-        copy.wait()
-    square = jnp.zeros((toks, 1), F32)
-    for start in range(0, width, 2 * PAIR):
-        tok = tok_sc[:, start : min(start + 2 * PAIR, width)].astype(F32)
-        square = square + jnp.sum(tok * tok, axis=1, keepdims=True)
-    inv = lax.rsqrt(square / width + norm_epsilon)
     chunks[0].wait()
 
     def put(at, value):
         nine_sc[:, at : at + LANE] = value
 
     get_tail(msg_sc, fold_sc, put, tail_at, tail, experts)
+    tok_copy.wait()
     along = jnp.zeros((toks, 1), F32)
     for copy, (at, size) in zip(chunks[1:], pieces[1:]):
         copy.wait()
         for start in range(at, min(at + size, width), 2 * PAIR):
             stop = min(start + 2 * PAIR, at + size, width)
-            total = mm(pick[:, :main], msg_sc[:, start:stop]) + mm(
-                pick[:, main:], nine_sc[:, start:stop]
+            total = mm(pick_ref[:, :main], msg_sc[:, start:stop]) + mm(
+                pick_ref[:, main:], nine_sc[:, start:stop]
             )
-            total = (total + dn_sc[:, start:stop]) * gain_ref[0:1, start:stop].astype(F32)
+            total = total * gain_ref[0:1, start:stop].astype(F32)
             sum_sc[:, start:stop] = total
             along = along + jnp.sum(total * tok_sc[:, start:stop].astype(F32), axis=1, keepdims=True)
+    base_copy.wait()
+    inv = inv_ref[:, 0:1]
     cube = inv * inv * inv * (along / width)
 
     def load(start, size):
         value = (
-            cot_sc[:, start : start + size].astype(F32)
+            base_sc[:, start : start + size]
             + inv * sum_sc[:, start : start + size]
             - tok_sc[:, start : start + size].astype(F32) * cube
         )
@@ -539,11 +554,11 @@
 
     table = struct((experts, toks), F32)
     block = struct((toks, width), BF16)
-    row_msg, prob, slot, tokp, gainp, routerp = simple_call(
+    row_msg, slot, tokp, gainp = simple_call(
         dispatch_rows_kernel,
-        (msg, table, table, block, struct((16, width), BF16), struct((experts, width), BF16)),
+        (msg, table, block, struct((16, width), BF16)),
         [pltpu.VMEM((toks, width), BF16), pltpu.VMEM((16, width), BF16), nine_f, fold],
-    )(tokens.T, norm_gain, router_weight.T, expert_ids.T)
+    )(tokens.T, norm_gain, expert_ids.T)
     row_msg, gate_up_words, down_words = lax.optimization_barrier(
         (row_msg, gate_up_words, down_words)
     )
@@ -554,9 +569,11 @@
         return swapped.reshape(rows, msg_width)
 
     rows_in = exchange(row_msg)
-    grad_msg, cotp = simple_call(
-        dispatch_grads_kernel, (msg, block), [nine_f, fold]
-    )(cotangent.T, prob, slot)
+    grad_msg, cotp, prob, routerp = simple_call(
+        dispatch_grads_kernel,
+        (msg, block, table, struct((experts, width), BF16)),
+        [pltpu.VMEM((toks, width), BF16), nine_f, fold],
+    )(cotangent.T, slot, tokp, gainp, router_weight.T)
     grads_in = exchange(grad_msg)
 
     group_rows = word_rows // gate_up_scales.shape[1]
@@ -660,29 +677,33 @@
     backs_in = exchange(back_msg)
 
     turned = struct((width, toks), BF16)
-    mixed, dnormed = simple_call(
+    mixed, base, pick, inv = simple_call(
         combine_out_kernel,
-        (turned, struct((toks, width), F32)),
+        (
+            turned,
+            struct((toks, width), F32),
+            struct((toks, all_rows), BF16),
+            struct((toks, LANE), F32),
+        ),
         [nine_b, fold, pltpu.VMEM((toks, width), BF16)],
-    )(outs_in, tokp, cotp, prob, slot, routerp)
+    )(outs_in, tokp, cotp, prob, slot, routerp, gainp)
     in_hbm, in_vmem = pl.BlockSpec(memory_space=pltpu.HBM), pl.BlockSpec(memory_space=pltpu.VMEM)
     token_grad = pl.pallas_call(
         combine_back_kernel,
         out_shape=turned,
-        in_specs=[in_hbm, in_hbm, in_hbm, in_vmem, in_vmem, in_hbm],
+        in_specs=[in_hbm, in_hbm, in_hbm, in_vmem, in_vmem, in_vmem],
         scratch_shapes=[
             nine_b,
             fold,
             pltpu.VMEM((toks, width), F32),
             pltpu.VMEM((rows, msg_width), BF16),
             pltpu.VMEM((toks, width), BF16),
-            pltpu.VMEM((toks, width), BF16),
             pltpu.VMEM((toks, width), F32),
-            pltpu.SemaphoreType.DMA((4 + -(-tail_at // (4 * PAIR)),)),
+            pltpu.SemaphoreType.DMA((3 + -(-tail_at // (4 * PAIR)),)),
         ],
         compiler_params=params(63),
         name="combine_back",
-    )(backs_in, tokp, cotp, slot, gainp, dnormed)
+    )(backs_in, tokp, base, pick, inv, gainp)
     return mixed.T, token_grad.T
 
 

time: 238 us -> 237 us (level)
  no operation moved by 1% of the time
where the time goes in v3:
time: 237 us; the launch traced here: 236 us
  Pallas kernels  120 us (51%)
  waiting for transfers between devices  82.7 us (35%)
  starting transfers between devices  29.3 us (12%)
  local copies, waits for them, and re-layouts  2.85 us (1%)
    all_to_all x4, waiting for transfers between devices, exchange(): swapped = lax.all_to_all(shaped, ('dp', 'x'), 0, 0, tiled=True)  82.7 us
    pallas_call x1, Pallas kernels, shards(): pl.pallas_call(functools.partial(ffn_forward_kernel, width=width, half=ha...  36.9 us
    pallas_call x1, Pallas kernels, shards(): pl.pallas_call(functools.partial(ffn_backward_kernel, width=width, half=h...  35.5 us
    all_to_all x4, starting transfers between devices, exchange(): swapped = lax.all_to_all(shaped, ('dp', 'x'), 0, 0, tiled=True)  29.1 us
    pallas_call x1, Pallas kernels, shards(): pl.pallas_call(functools.partial(decode_rows_kernel, word_rows - (steps -...  14.5 us
    pallas_call x1, Pallas kernels, shards(): pl.pallas_call(decode_cols_kernel, out_shape=struct((half, 2 * word_cols)...  8.87 us
    pallas_call x1, Pallas kernels, shards(): simple_call(combine_out_kernel, (turned, struct((toks, width), F32), stru...  8.81 us
    pallas_call x1, Pallas kernels, shards(): pl.pallas_call(combine_back_kernel, out_shape=turned, in_specs=[in_hbm, i...  5.5 us
  transfers between devices with their start and end apart: 6, of which 4 were waited for; matrix products, arithmetic and copies ran while one was open for 0% of the time, Pallas kernels for 40%

profile of v3, /device:TPU:0, one launch (start us, length us, event | category | flops | bytes accessed | tf_op | source)
XLA Modules:
  0.0 235.6 jit_solution(4926952343899242806)
XLA Ops:
  0.6 4.6 %shard_map.104 = (bf16[512,3328]{1,0:T(8,128)(2,1)}, f32[64,128]{1,0:T(8,128)}, bf16[128,2880]{1,0:T(8,128)(2,1)}, bf16[16,2880]{1,0:T(8,128)(2,1)}) custom-call(bf16[2880,128]{1,0:T(8,128)(2,1)} %bitcast.28, bf16[2880]{0:T(1024)(128)(2,1)} %gain_ref.1, s32[4,128]{1,0:T(4,128)} %bitcast.32), custom_call_target="tpu_custom_call" | custom-call | tf_op jit(solution)/shard_map/pallas_call | solution.py:557
  5.3 1.9 copy.14
  7.2 14.5 %decode_gate_up.1.gu_own_ref = bf16[2880,1536]{1,0:T(8,128)(2,1)} custom-call(s32[1440,1440]{1,0:T(8,128)} %bitcast.21, s32[90,1440]{1,0:T(8,128)} %bitcast.26), custom_call_target="tpu_custom_call" | custom-call | tf_op jit(solution)/shard_map/decode_gate_up/pallas_call | solution.py:581
  21.6 0.0 collective-permute-start
  21.6 0.0 copy-start
  21.6 11.9 %all-to-all-start = ((bf16[64,8,3328]{2,1,0:T(8,128)(2,1)}), bf16[64,8,3328]{2,1,0:T(8,128)(2,1)}, u32[]{:S(2)}, u32[]{:S(2)}) async-start(bf16[64,8,3328]{2,1,0:T(8,128)(2,1)} %bitcast.23), calls=%async_computation | async-start | bytes 6815744 | tf_op jit(solution)/shard_map/all_to_all | solution.py:568
  33.5 0.0 copy-done
  33.6 0.9 copy.11
  34.5 8.9 %decode_down.1.down_own_ref = bf16[720,2880]{1,0:T(8,128)(2,1)} custom-call(s32[720,1440]{1,0:T(8,128)} %bitcast.22, s32[720,90]{1,0:T(8,128)} %bitcast.27), custom_call_target="tpu_custom_call" | custom-call | tf_op jit(solution)/shard_map/decode_down/pallas_call | solution.py:595
  43.4 0.2 collective-permute-start.1
  43.6 5.2 %shard_map.105 = (bf16[512,3328]{1,0:T(8,128)(2,1)}, bf16[128,2880]{1,0:T(8,128)(2,1)}, f32[64,128]{1,0:T(8,128)}, bf16[64,2880]{1,0:T(8,128)(2,1)}) custom-call(bf16[2880,128]{1,0:T(8,128)(2,1)} %bitcast.30, f32[64,128]{1,0:T(8,128)} %get-tuple-element.26.slot_ref, bf16[128,2880]{1,0:T(8,128)(2,1)} %get-tuple-element.25.tokp_ref, ...), custom_call_target="tpu_custom_call" | custom-call | tf_op jit(solution)/shard_map/pallas_call | solution.py:572
  48.8 31.0 %all-to-all-done = bf16[64,8,3328]{2,1,0:T(8,128)(2,1)} async-done(((bf16[64,8,3328]{2,1,0:T(8,128)(2,1)}), bf16[64,8,3328]{2,1,0:T(8,128)(2,1)}, u32[]{:S(2)}, u32[]{:S(2)}) %all-to-all-start) | async-done | bytes 3407904 | tf_op jit(solution)/shard_map/all_to_all | solution.py:568
  79.8 5.6 %all-to-all-start.2 = ((bf16[64,8,3328]{2,1,0:T(8,128)(2,1)}), bf16[64,8,3328]{2,1,0:T(8,128)(2,1)}, u32[]{:S(2)}, u32[]{:S(2)}) async-start(bf16[64,8,3328]{2,1,0:T(8,128)(2,1)} %bitcast.24), calls=%async_computation.2 | async-start | bytes 6815744 | tf_op jit(solution)/shard_map/all_to_all | solution.py:568
  85.4 0.0 collective-permute-done.1.down_oth_ref
  85.4 0.0 collective-permute-done.gu_oth_ref
  85.4 36.9 %ffn_forward.1 = (bf16[512,3328]{1,0:T(8,128)(2,1)}, f32[576,1536]{1,0:T(8,128)}, f32[576,1536]{1,0:T(8,128)}) custom-call(bf16[512,3328]{1,0:T(8,128)(2,1)} %bitcast.3.x_ref, bf16[2880,1536]{1,0:T(8,128)(2,1)} %decode_gate_up.1.gu_own_ref, bf16[2880,1536]{1,0:T(8,128)(2,1)} %collective-permute-done.gu_oth_ref, bf16[720,2880]{1,0:T(8,128)(2,1)} %decode_down.1.down_own_ref, ...), custom_call_target="tpu_custom_call" | custom-call | tf_op jit(solution)/shard_map/ffn_forward/pallas_call | solution.py:621
  122.3 8.0 %all-to-all-done.2 = bf16[64,8,3328]{2,1,0:T(8,128)(2,1)} async-done(((bf16[64,8,3328]{2,1,0:T(8,128)(2,1)}), bf16[64,8,3328]{2,1,0:T(8,128)(2,1)}, u32[]{:S(2)}, u32[]{:S(2)}) %all-to-all-start.2) | async-done | bytes 3407904 | tf_op jit(solution)/shard_map/all_to_all | solution.py:568
  130.3 5.8 %all-to-all-start.1 = ((bf16[64,8,3328]{2,1,0:T(8,128)(2,1)}), bf16[64,8,3328]{2,1,0:T(8,128)(2,1)}, u32[]{:S(2)}, u32[]{:S(2)}) async-start(bf16[64,8,3328]{2,1,0:T(8,128)(2,1)} %bitcast.25), calls=%async_computation.1 | async-start | bytes 6815744 | tf_op jit(solution)/shard_map/all_to_all | solution.py:568
  136.0 35.5 %ffn_backward.1 = bf16[512,3328]{1,0:T(8,128)(2,1)} custom-call(bf16[512,3328]{1,0:T(8,128)(2,1)} %bitcast.13.g_ref, f32[576,1536]{1,0:T(8,128)} %get-tuple-element.33.coef_own_ref, f32[576,1536]{1,0:T(8,128)} %get-tuple-element.34.coef_oth_ref, bf16[720,2880]{1,0:T(8,128)(2,1)} %decode_down.1.down_own_ref, ...), custom_call_target="tpu_custom_call" | custom-call | tf_op jit(solution)/shard_map/ffn_backward/pallas_call | solution.py:648
  171.6 9.5 %all-to-all-done.1 = bf16[64,8,3328]{2,1,0:T(8,128)(2,1)} async-done(((bf16[64,8,3328]{2,1,0:T(8,128)(2,1)}), bf16[64,8,3328]{2,1,0:T(8,128)(2,1)}, u32[]{:S(2)}, u32[]{:S(2)}) %all-to-all-start.1) | async-done | bytes 3407904 | tf_op jit(solution)/shard_map/all_to_all | solution.py:568
  181.1 5.8 %all-to-all-start.3 = ((bf16[64,8,3328]{2,1,0:T(8,128)(2,1)}), bf16[64,8,3328]{2,1,0:T(8,128)(2,1)}, u32[]{:S(2)}, u32[]{:S(2)}) async-start(bf16[64,8,3328]{2,1,0:T(8,128)(2,1)} %bitcast.20), calls=%async_computation.3 | async-start | bytes 6815744 | tf_op jit(solution)/shard_map/all_to_all | solution.py:568
  186.9 8.8 %shard_map.106 = (bf16[2880,128]{1,0:T(8,128)(2,1)}, f32[128,2880]{1,0:T(8,128)}, bf16[128,576]{1,0:T(8,128)(2,1)}, f32[128,128]{1,0:T(8,128)}) custom-call(bf16[512,3328]{1,0:T(8,128)(2,1)} %bitcast.8.msg_ref, bf16[128,2880]{1,0:T(8,128)(2,1)} %get-tuple-element.25.tokp_ref, bf16[128,2880]{1,0:T(8,128)(2,1)} %get-tuple-element.28.cotp_ref, ...), custom_call_target="tpu_custom_call" | custom-call | tf_op jit(solution)/shard_map/pallas_call | solution.py:680
  195.7 34.2 %all-to-all-done.3 = bf16[64,8,3328]{2,1,0:T(8,128)(2,1)} async-done(((bf16[64,8,3328]{2,1,0:T(8,128)(2,1)}), bf16[64,8,3328]{2,1,0:T(8,128)(2,1)}, u32[]{:S(2)}, u32[]{:S(2)}) %all-to-all-start.3) | async-done | bytes 3407904 | tf_op jit(solution)/shard_map/all_to_all | solution.py:568
  229.9 5.5 %combine_back.1 = bf16[2880,128]{1,0:T(8,128)(2,1)} custom-call(bf16[512,3328]{1,0:T(8,128)(2,1)} %bitcast.15.msg_ref, bf16[128,2880]{1,0:T(8,128)(2,1)} %get-tuple-element.25.tokp_ref, f32[128,2880]{1,0:T(8,128)} %get-tuple-element.35.base_ref, bf16[128,576]{1,0:T(8,128)(2,1)} %get-tuple-element.36.pick_ref, f32[128,128]{1,0:T(8,128)} %get-tuple-element.37.inv_ref, ...), custom_call_target="tpu_custom_call" | custom-call | tf_op jit(solution)/shard_map/combine_back/pallas_call | solution.py:691
Async XLA Ops:
  21.6 63.8 %collective-permute-start = (bf16[2880,1536]{1,0:T(8,128)(2,1)}, bf16[2880,1536]{1,0:T(8,128)(2,1)}, u32[]{:S(2)}, u32[]{:S(2)}) collective-permute-start(bf16[2880,1536]{1,0:T(8,128)(2,1)} %decode_gate_up.1.gu_own_ref), channel_id=1, source_target_pairs={{0,1},{1,0},{2,3},{3,2},{4,5},{5,4},{6,7},{7,6},{8,9},{9,8},{10,11... | collective-permute-start | bytes 26542088 | tf_op jit(solution)/shard_map/ppermute | solution.py:609
  21.6 11.9 %copy-start = (s32[1,720,90]{1,0,2:T(1,128)S(1)}, s32[1,720,90]{1,0,2:T(1,128)}, u32[]{:S(2)}) copy-start(s32[1,720,90]{1,0,2:T(1,128)} %param.16) | copy-start | bytes 777604
  21.6 58.2 %all-to-all-start = ((bf16[64,8,3328]{2,1,0:T(8,128)(2,1)}), bf16[64,8,3328]{2,1,0:T(8,128)(2,1)}, u32[]{:S(2)}, u32[]{:S(2)}) async-start(bf16[64,8,3328]{2,1,0:T(8,128)(2,1)} %bitcast.23), calls=%async_computation | async-start | bytes 6815744 | tf_op jit(solution)/shard_map/all_to_all | solution.py:568
  43.4 42.0 %collective-permute-start.1 = (bf16[720,2880]{1,0:T(8,128)(2,1)}, bf16[720,2880]{1,0:T(8,128)(2,1)}, u32[]{:S(2)}, u32[]{:S(2)}) collective-permute-start(bf16[720,2880]{1,0:T(8,128)(2,1)} %decode_down.1.down_own_ref), channel_id=1, source_target_pairs={{0,1},{1,0},{2,3},{3,2},{4,5},{5,4},{6,7},{7,6},{8,9},{9,8},{10,11... | collective-permute-start | bytes 12441608 | tf_op jit(solution)/shard_map/ppermute | solution.py:610
  79.8 50.5 %all-to-all-start.2 = ((bf16[64,8,3328]{2,1,0:T(8,128)(2,1)}), bf16[64,8,3328]{2,1,0:T(8,128)(2,1)}, u32[]{:S(2)}, u32[]{:S(2)}) async-start(bf16[64,8,3328]{2,1,0:T(8,128)(2,1)} %bitcast.24), calls=%async_computation.2 | async-start | bytes 6815744 | tf_op jit(solution)/shard_map/all_to_all | solution.py:568
  130.3 50.8 %all-to-all-start.1 = ((bf16[64,8,3328]{2,1,0:T(8,128)(2,1)}), bf16[64,8,3328]{2,1,0:T(8,128)(2,1)}, u32[]{:S(2)}, u32[]{:S(2)}) async-start(bf16[64,8,3328]{2,1,0:T(8,128)(2,1)} %bitcast.25), calls=%async_computation.1 | async-start | bytes 6815744 | tf_op jit(solution)/shard_map/all_to_all | solution.py:568
  181.1 48.9 %all-to-all-start.3 = ((bf16[64,8,3328]{2,1,0:T(8,128)(2,1)}), bf16[64,8,3328]{2,1,0:T(8,128)(2,1)}, u32[]{:S(2)}, u32[]{:S(2)}) async-start(bf16[64,8,3328]{2,1,0:T(8,128)(2,1)} %bitcast.20), calls=%async_computation.3 | async-start | bytes 6815744 | tf_op jit(solution)/shard_map/all_to_all | solution.py:568

commit v4 on v3

--- a/solution.py
+++ b/solution.py
@@ -135,7 +135,7 @@
 def dispatch_rows_kernel(
     tok_ref, gain_ref, ids_ref,
     msg_ref, slot_ref, tokp_ref, gainp_ref,
-    normp_sc, gain_sc, nine_sc, fold_sc,
+    normp_sc, gain_sc, nine_sc, fold_sc, msg_sc, sem,
 ):
     width, toks = tok_ref.shape
     top = ids_ref.shape[0]
@@ -155,12 +155,28 @@
     slot_ref[...] = slot
     hot, hot_nine = slot_hot(slot)
     hot = hot.astype(BF16)
-    for start in range(0, width, 2 * PAIR):
-        stop = min(start + 2 * PAIR, width)
-        msg_ref[:, start:stop] = mm(hot, normp_sc[:, start:stop]).astype(BF16)
-    msg_ref[:, width:tail_at] = jnp.zeros((msg_ref.shape[0], tail_at - width), BF16)
+    step = 2 * PAIR
+    count = width // step
+
+    def fill(start, stop):
+        msg_sc[:, start:stop] = mm(hot, normp_sc[:, start:stop]).astype(BF16)
+
+    def send(index, start, size):
+        at = pl.ds(start, size)
+        copy = pltpu.make_async_copy(msg_sc.at[:, at], msg_ref.at[:, at], sem.at[index])
+        copy.start()
+        return copy
+
+    fill(count * step, width)
+    msg_sc[:, width:tail_at] = jnp.zeros((msg_sc.shape[0], tail_at - width), BF16)
     nine = mm(hot_nine.astype(BF16), normp_sc[...])
-    put_tail(msg_ref, nine, nine_sc, fold_sc, tail_at, tail, width)
+    put_tail(msg_sc, nine, nine_sc, fold_sc, tail_at, tail, width)
+    copies = [send(count, count * step, tail_at + tail - count * step)]
+    for i in range(count):
+        fill(i * step, (i + 1) * step)
+        copies.append(send(i, i * step, step))
+    for copy in copies:
+        copy.wait()
 
 
 def dispatch_grads_kernel(
@@ -554,10 +570,22 @@
 
     table = struct((experts, toks), F32)
     block = struct((toks, width), BF16)
-    row_msg, slot, tokp, gainp = simple_call(
+    in_hbm, in_vmem = pl.BlockSpec(memory_space=pltpu.HBM), pl.BlockSpec(memory_space=pltpu.VMEM)
+    row_msg, slot, tokp, gainp = pl.pallas_call(
         dispatch_rows_kernel,
-        (msg, table, block, struct((16, width), BF16)),
-        [pltpu.VMEM((toks, width), BF16), pltpu.VMEM((16, width), BF16), nine_f, fold],
+        out_shape=(msg, table, block, struct((16, width), BF16)),
+        in_specs=[in_vmem] * 3,
+        out_specs=(in_hbm, in_vmem, in_vmem, in_vmem),
+        scratch_shapes=[
+            pltpu.VMEM((toks, width), BF16),
+            pltpu.VMEM((16, width), BF16),
+            nine_f,
+            fold,
+            pltpu.VMEM((rows, msg_width), BF16),
+            pltpu.SemaphoreType.DMA((1 + width // (2 * PAIR),)),
+        ],
+        compiler_params=params(63),
+        name="dispatch_rows",
     )(tokens.T, norm_gain, expert_ids.T)
     row_msg, gate_up_words, down_words = lax.optimization_barrier(
         (row_msg, gate_up_words, down_words)

time: 237 us -> 237 us (level)
  no operation moved by 1% of the time
where the time goes in v4:
time: 237 us; the launch traced here: 236 us
  Pallas kernels  120 us (51%)
  waiting for transfers between devices  82.7 us (35%)
  starting transfers between devices  29.3 us (12%)
  local copies, waits for them, and re-layouts  2.85 us (1%)
    all_to_all x4, waiting for transfers between devices, exchange(): swapped = lax.all_to_all(shaped, ('dp', 'x'), 0, 0, tiled=True)  82.7 us
    pallas_call x1, Pallas kernels, shards(): pl.pallas_call(functools.partial(ffn_forward_kernel, width=width, half=ha...  36.9 us
    pallas_call x1, Pallas kernels, shards(): pl.pallas_call(functools.partial(ffn_backward_kernel, width=width, half=h...  35.5 us
    all_to_all x4, starting transfers between devices, exchange(): swapped = lax.all_to_all(shaped, ('dp', 'x'), 0, 0, tiled=True)  29.1 us
    pallas_call x1, Pallas kernels, shards(): pl.pallas_call(functools.partial(decode_rows_kernel, word_rows - (steps -...  14.5 us
    pallas_call x1, Pallas kernels, shards(): pl.pallas_call(decode_cols_kernel, out_shape=struct((half, 2 * word_cols)...  8.87 us
    pallas_call x1, Pallas kernels, shards(): simple_call(combine_out_kernel, (turned, struct((toks, width), F32), stru...  8.81 us
    pallas_call x1, Pallas kernels, shards(): pl.pallas_call(combine_back_kernel, out_shape=turned, in_specs=[in_hbm, i...  5.5 us
  transfers between devices with their start and end apart: 6, of which 4 were waited for; matrix products, arithmetic and copies ran while one was open for 0% of the time, Pallas kernels for 40%

profile of v4, /device:TPU:0, one launch (start us, length us, event | category | flops | bytes accessed | tf_op | source)
XLA Modules:
  0.0 236.1 jit_solution(14120270771600621082)
XLA Ops:
  0.6 5.1 %dispatch_rows.1 = (bf16[512,3328]{1,0:T(8,128)(2,1)}, f32[64,128]{1,0:T(8,128)}, bf16[128,2880]{1,0:T(8,128)(2,1)}, bf16[16,2880]{1,0:T(8,128)(2,1)}) custom-call(bf16[2880,128]{1,0:T(8,128)(2,1)} %bitcast.28, bf16[2880]{0:T(1024)(128)(2,1)} %gain_ref.1, s32[4,128]{1,0:T(4,128)} %bitcast.32), custom_call_target="tpu_custom_call" | custom-call | tf_op jit(solution)/shard_map/dispatch_rows/pallas_call | solution.py:574
  5.7 1.9 copy.14
  7.6 14.5 %decode_gate_up.1.gu_own_ref = bf16[2880,1536]{1,0:T(8,128)(2,1)} custom-call(s32[1440,1440]{1,0:T(8,128)} %bitcast.21, s32[90,1440]{1,0:T(8,128)} %bitcast.26), custom_call_target="tpu_custom_call" | custom-call | tf_op jit(solution)/shard_map/decode_gate_up/pallas_call | solution.py:609
  22.1 0.0 collective-permute-start
  22.1 0.0 copy-start
  22.1 11.9 %all-to-all-start = ((bf16[64,8,3328]{2,1,0:T(8,128)(2,1)}), bf16[64,8,3328]{2,1,0:T(8,128)(2,1)}, u32[]{:S(2)}, u32[]{:S(2)}) async-start(bf16[64,8,3328]{2,1,0:T(8,128)(2,1)} %bitcast.23), calls=%async_computation | async-start | bytes 6815744 | tf_op jit(solution)/shard_map/all_to_all | solution.py:596
  34.0 0.0 copy-done
  34.0 0.9 copy.11
  34.9 8.9 %decode_down.1.down_own_ref = bf16[720,2880]{1,0:T(8,128)(2,1)} custom-call(s32[720,1440]{1,0:T(8,128)} %bitcast.22, s32[720,90]{1,0:T(8,128)} %bitcast.27), custom_call_target="tpu_custom_call" | custom-call | tf_op jit(solution)/shard_map/decode_down/pallas_call | solution.py:623
  43.8 0.2 collective-permute-start.1
  44.0 5.2 %shard_map.104 = (bf16[512,3328]{1,0:T(8,128)(2,1)}, bf16[128,2880]{1,0:T(8,128)(2,1)}, f32[64,128]{1,0:T(8,128)}, bf16[64,2880]{1,0:T(8,128)(2,1)}) custom-call(bf16[2880,128]{1,0:T(8,128)(2,1)} %bitcast.30, f32[64,128]{1,0:T(8,128)} %get-tuple-element.26.slot_ref, bf16[128,2880]{1,0:T(8,128)(2,1)} %get-tuple-element.25.tokp_ref, ...), custom_call_target="tpu_custom_call" | custom-call | tf_op jit(solution)/shard_map/pallas_call | solution.py:600
  49.2 31.0 %all-to-all-done = bf16[64,8,3328]{2,1,0:T(8,128)(2,1)} async-done(((bf16[64,8,3328]{2,1,0:T(8,128)(2,1)}), bf16[64,8,3328]{2,1,0:T(8,128)(2,1)}, u32[]{:S(2)}, u32[]{:S(2)}) %all-to-all-start) | async-done | bytes 3407904 | tf_op jit(solution)/shard_map/all_to_all | solution.py:596
  80.2 5.6 %all-to-all-start.2 = ((bf16[64,8,3328]{2,1,0:T(8,128)(2,1)}), bf16[64,8,3328]{2,1,0:T(8,128)(2,1)}, u32[]{:S(2)}, u32[]{:S(2)}) async-start(bf16[64,8,3328]{2,1,0:T(8,128)(2,1)} %bitcast.24), calls=%async_computation.2 | async-start | bytes 6815744 | tf_op jit(solution)/shard_map/all_to_all | solution.py:596
  85.8 0.0 collective-permute-done.1.down_oth_ref
  85.8 0.0 collective-permute-done.gu_oth_ref
  85.9 36.9 %ffn_forward.1 = (bf16[512,3328]{1,0:T(8,128)(2,1)}, f32[576,1536]{1,0:T(8,128)}, f32[576,1536]{1,0:T(8,128)}) custom-call(bf16[512,3328]{1,0:T(8,128)(2,1)} %bitcast.3.x_ref, bf16[2880,1536]{1,0:T(8,128)(2,1)} %decode_gate_up.1.gu_own_ref, bf16[2880,1536]{1,0:T(8,128)(2,1)} %collective-permute-done.gu_oth_ref, bf16[720,2880]{1,0:T(8,128)(2,1)} %decode_down.1.down_own_ref, ...), custom_call_target="tpu_custom_call" | custom-call | tf_op jit(solution)/shard_map/ffn_forward/pallas_call | solution.py:649
  122.7 8.0 %all-to-all-done.2 = bf16[64,8,3328]{2,1,0:T(8,128)(2,1)} async-done(((bf16[64,8,3328]{2,1,0:T(8,128)(2,1)}), bf16[64,8,3328]{2,1,0:T(8,128)(2,1)}, u32[]{:S(2)}, u32[]{:S(2)}) %all-to-all-start.2) | async-done | bytes 3407904 | tf_op jit(solution)/shard_map/all_to_all | solution.py:596
  130.7 5.8 %all-to-all-start.1 = ((bf16[64,8,3328]{2,1,0:T(8,128)(2,1)}), bf16[64,8,3328]{2,1,0:T(8,128)(2,1)}, u32[]{:S(2)}, u32[]{:S(2)}) async-start(bf16[64,8,3328]{2,1,0:T(8,128)(2,1)} %bitcast.25), calls=%async_computation.1 | async-start | bytes 6815744 | tf_op jit(solution)/shard_map/all_to_all | solution.py:596
  136.5 35.5 %ffn_backward.1 = bf16[512,3328]{1,0:T(8,128)(2,1)} custom-call(bf16[512,3328]{1,0:T(8,128)(2,1)} %bitcast.13.g_ref, f32[576,1536]{1,0:T(8,128)} %get-tuple-element.33.coef_own_ref, f32[576,1536]{1,0:T(8,128)} %get-tuple-element.34.coef_oth_ref, bf16[720,2880]{1,0:T(8,128)(2,1)} %decode_down.1.down_own_ref, ...), custom_call_target="tpu_custom_call" | custom-call | tf_op jit(solution)/shard_map/ffn_backward/pallas_call | solution.py:676
  172.0 9.5 %all-to-all-done.1 = bf16[64,8,3328]{2,1,0:T(8,128)(2,1)} async-done(((bf16[64,8,3328]{2,1,0:T(8,128)(2,1)}), bf16[64,8,3328]{2,1,0:T(8,128)(2,1)}, u32[]{:S(2)}, u32[]{:S(2)}) %all-to-all-start.1) | async-done | bytes 3407904 | tf_op jit(solution)/shard_map/all_to_all | solution.py:596
  181.5 5.8 %all-to-all-start.3 = ((bf16[64,8,3328]{2,1,0:T(8,128)(2,1)}), bf16[64,8,3328]{2,1,0:T(8,128)(2,1)}, u32[]{:S(2)}, u32[]{:S(2)}) async-start(bf16[64,8,3328]{2,1,0:T(8,128)(2,1)} %bitcast.20), calls=%async_computation.3 | async-start | bytes 6815744 | tf_op jit(solution)/shard_map/all_to_all | solution.py:596
  187.3 8.8 %shard_map.105 = (bf16[2880,128]{1,0:T(8,128)(2,1)}, f32[128,2880]{1,0:T(8,128)}, bf16[128,576]{1,0:T(8,128)(2,1)}, f32[128,128]{1,0:T(8,128)}) custom-call(bf16[512,3328]{1,0:T(8,128)(2,1)} %bitcast.8.msg_ref, bf16[128,2880]{1,0:T(8,128)(2,1)} %get-tuple-element.25.tokp_ref, bf16[128,2880]{1,0:T(8,128)(2,1)} %get-tuple-element.28.cotp_ref, ...), custom_call_target="tpu_custom_call" | custom-call | tf_op jit(solution)/shard_map/pallas_call | solution.py:708
  196.2 34.2 %all-to-all-done.3 = bf16[64,8,3328]{2,1,0:T(8,128)(2,1)} async-done(((bf16[64,8,3328]{2,1,0:T(8,128)(2,1)}), bf16[64,8,3328]{2,1,0:T(8,128)(2,1)}, u32[]{:S(2)}, u32[]{:S(2)}) %all-to-all-start.3) | async-done | bytes 3407904 | tf_op jit(solution)/shard_map/all_to_all | solution.py:596
  230.4 5.5 %combine_back.1 = bf16[2880,128]{1,0:T(8,128)(2,1)} custom-call(bf16[512,3328]{1,0:T(8,128)(2,1)} %bitcast.15.msg_ref, bf16[128,2880]{1,0:T(8,128)(2,1)} %get-tuple-element.25.tokp_ref, f32[128,2880]{1,0:T(8,128)} %get-tuple-element.35.base_ref, bf16[128,576]{1,0:T(8,128)(2,1)} %get-tuple-element.36.pick_ref, f32[128,128]{1,0:T(8,128)} %get-tuple-element.37.inv_ref, ...), custom_call_target="tpu_custom_call" | custom-call | tf_op jit(solution)/shard_map/combine_back/pallas_call | solution.py:719
Async XLA Ops:
  22.1 63.8 %collective-permute-start = (bf16[2880,1536]{1,0:T(8,128)(2,1)}, bf16[2880,1536]{1,0:T(8,128)(2,1)}, u32[]{:S(2)}, u32[]{:S(2)}) collective-permute-start(bf16[2880,1536]{1,0:T(8,128)(2,1)} %decode_gate_up.1.gu_own_ref), channel_id=1, source_target_pairs={{0,1},{1,0},{2,3},{3,2},{4,5},{5,4},{6,7},{7,6},{8,9},{9,8},{10,11... | collective-permute-start | bytes 26542088 | tf_op jit(solution)/shard_map/ppermute | solution.py:637
  22.1 11.9 %copy-start = (s32[1,720,90]{1,0,2:T(1,128)S(1)}, s32[1,720,90]{1,0,2:T(1,128)}, u32[]{:S(2)}) copy-start(s32[1,720,90]{1,0,2:T(1,128)} %param.16) | copy-start | bytes 777604
  22.1 58.2 %all-to-all-start = ((bf16[64,8,3328]{2,1,0:T(8,128)(2,1)}), bf16[64,8,3328]{2,1,0:T(8,128)(2,1)}, u32[]{:S(2)}, u32[]{:S(2)}) async-start(bf16[64,8,3328]{2,1,0:T(8,128)(2,1)} %bitcast.23), calls=%async_computation | async-start | bytes 6815744 | tf_op jit(solution)/shard_map/all_to_all | solution.py:596
  43.8 42.0 %collective-permute-start.1 = (bf16[720,2880]{1,0:T(8,128)(2,1)}, bf16[720,2880]{1,0:T(8,128)(2,1)}, u32[]{:S(2)}, u32[]{:S(2)}) collective-permute-start(bf16[720,2880]{1,0:T(8,128)(2,1)} %decode_down.1.down_own_ref), channel_id=1, source_target_pairs={{0,1},{1,0},{2,3},{3,2},{4,5},{5,4},{6,7},{7,6},{8,9},{9,8},{10,11... | collective-permute-start | bytes 12441608 | tf_op jit(solution)/shard_map/ppermute | solution.py:638
  80.2 50.5 %all-to-all-start.2 = ((bf16[64,8,3328]{2,1,0:T(8,128)(2,1)}), bf16[64,8,3328]{2,1,0:T(8,128)(2,1)}, u32[]{:S(2)}, u32[]{:S(2)}) async-start(bf16[64,8,3328]{2,1,0:T(8,128)(2,1)} %bitcast.24), calls=%async_computation.2 | async-start | bytes 6815744 | tf_op jit(solution)/shard_map/all_to_all | solution.py:596
  130.7 50.8 %all-to-all-start.1 = ((bf16[64,8,3328]{2,1,0:T(8,128)(2,1)}), bf16[64,8,3328]{2,1,0:T(8,128)(2,1)}, u32[]{:S(2)}, u32[]{:S(2)}) async-start(bf16[64,8,3328]{2,1,0:T(8,128)(2,1)} %bitcast.25), calls=%async_computation.1 | async-start | bytes 6815744 | tf_op jit(solution)/shard_map/all_to_all | solution.py:596
  181.5 48.9 %all-to-all-start.3 = ((bf16[64,8,3328]{2,1,0:T(8,128)(2,1)}), bf16[64,8,3328]{2,1,0:T(8,128)(2,1)}, u32[]{:S(2)}, u32[]{:S(2)}) async-start(bf16[64,8,3328]{2,1,0:T(8,128)(2,1)} %bitcast.20), calls=%async_computation.3 | async-start | bytes 6815744 | tf_op jit(solution)/shard_map/all_to_all | solution.py:596
